TPU v7x, 32 devices: a whole 2x2x4 slice. The times are simulated.
32 devices in a mesh: dp: 4 (over y, core), fsdp: 8 (over z, x).
Axes of the slice: x: 2, y: 2, z: 4, core: 2. Of those that a mesh axis runs over, the one named last changes fastest.
Arguments:
- signal: bfloat16 [256, 64, 4096], P(('dp', 'fsdp')), may hold values from -6 to 6
- segments: int32 [256, 4096], P(('dp', 'fsdp')), may hold values from 0 to 3, never falling along the last dimension, each value on 1 to 2048 neighbouring positions
- cotangent: bfloat16 [256, 32, 8192], P(('dp', 'fsdp')), may hold values from -6 to 6
- upsample_direction: bfloat16 [64, 128], P('dp', 'fsdp'), may hold values from -0.5 to 0.5
- upsample_gain: bfloat16 [64], P('fsdp'), may hold values from 0.5 to 2
- upsample_bias: bfloat16 [32], P('fsdp'), may hold values from -1.5 to 1.5
- dilated_direction: bfloat16 [3, 32, 96], P(None, 'dp', 'fsdp'), may hold values from -0.625 to 0.625
- paired_direction: bfloat16 [3, 2, 32, 32], P(None, None, 'dp', 'fsdp'), may hold values from -1 to 1
- residual_gain: bfloat16 [3, 3, 32], P(None, None, 'fsdp'), may hold values from 0.3984375 to 1.1953125
- residual_bias: bfloat16 [3, 3, 32], P(None, None, 'fsdp'), may hold values from -1.5 to 1.5
Outputs:
- output: bfloat16 [256, 32, 8192], P(('dp', 'fsdp'))
- signal_grad: bfloat16 [256, 64, 4096], P(('dp', 'fsdp'))
- up_dir_grad: float32 [64, 128], P('dp', 'fsdp')
- up_gain_grad: float32 [64], P('fsdp')
- up_bias_grad: float32 [32], P('fsdp')
- dil_dir_grad: float32 [3, 32, 96], P(None, 'dp', 'fsdp')
- pair_dir_grad: float32 [3, 2, 32, 32], P(None, None, 'dp', 'fsdp')
- res_gain_grad: float32 [3, 3, 32], P(None, None, 'fsdp')
- res_bias_grad: float32 [3, 3, 32], P(None, None, 'fsdp')
Inputs may be any that keep to these rules, and one draw needn't show every extreme that they name: `segments`: utterance numbers never fall along a row; each utterance is 1 to 2048 input samples long, one exactly that long.
All inputs are finite; a program needn't handle non-finite values.
Results may differ from a plain program's by a relative error of at most 0.017.
Values may be sent and summed in bfloat16 or wider, within the bound.
A program may use at most 384 MiB of HBM per device.

v0:
```python
import jax
import jax.numpy as jnp
from jax import lax
from jax.sharding import PartitionSpec as P

CHANNELS_OUT = 32
KERNEL = 4
RESIDUAL_BLOCKS = 3


def leaky_smooth(value):
    return 0.2 * value + 0.8 * jax.nn.silu(value)


def negative_slope(value):
    sigm = jax.nn.sigmoid(value)
    return 0.2 + 0.8 * (sigm + value * sigm * (1.0 - sigm))


def shifted(values, offset):
    length = values.shape[-1]
    zeros = jnp.zeros(values.shape[:-1] + (abs(offset),), values.dtype)
    if offset > 0:
        return jnp.concatenate([values[..., offset:], zeros], axis=-1)
    return jnp.concatenate([zeros, values[..., : length + offset]], axis=-1)


def same_seg(segment_index, offset):
    tagged = segment_index + 1
    return (shifted(tagged, offset) == tagged).astype(jnp.float32)


def gather_shards(
    upsample_direction,
    upsample_gain,
    upsample_bias,
    dilated_direction,
    paired_direction,
    residual_gain,
    residual_bias,
):
    inner = (
        lax.all_gather(upsample_direction, "fsdp", axis=1, tiled=True),
        lax.all_gather(dilated_direction, "fsdp", axis=2, tiled=True),
        lax.all_gather(paired_direction, "fsdp", axis=3, tiled=True),
        lax.all_gather(upsample_gain, "fsdp", axis=0, tiled=True),
        lax.all_gather(upsample_bias, "fsdp", axis=0, tiled=True),
        lax.all_gather(residual_gain, "fsdp", axis=2, tiled=True),
        lax.all_gather(residual_bias, "fsdp", axis=2, tiled=True),
    )
    outer = (
        lax.all_gather(inner[0], "dp", axis=0, tiled=True),
        lax.all_gather(inner[1], "dp", axis=1, tiled=True),
        lax.all_gather(inner[2], "dp", axis=2, tiled=True),
    )
    return (outer[0], inner[3], inner[4], outer[1], outer[2], inner[5], inner[6])


def prepare(fetched):
    (
        upsample_direction,
        upsample_gain,
        upsample_bias,
        dilated_direction,
        paired_direction,
        residual_gain,
        residual_bias,
    ) = [block_item.astype(jnp.float32) for block_item in fetched]
    up_norm = jnp.sqrt(jnp.sum(upsample_direction * upsample_direction, axis=1, keepdims=True))
    up_scale = upsample_gain[:, None]
    dilated_row_norm = jnp.sqrt(
        jnp.sum(dilated_direction * dilated_direction, axis=2, keepdims=True)
    )
    dilated_row_scale = residual_gain[:, 0, :, None]
    pair_norm = jnp.sqrt(jnp.sum(paired_direction * paired_direction, axis=3, keepdims=True))
    pair_scale = residual_gain[:, 1:, :, None]
    upsample_weight = (up_scale * upsample_direction / up_norm).astype(jnp.bfloat16)
    dilated_kernel_weight = (dilated_row_scale * dilated_direction / dilated_row_norm).astype(
        jnp.bfloat16
    )
    paired_kernel_weight = (pair_scale * paired_direction / pair_norm).astype(jnp.bfloat16)
    weight_rows = (
        (upsample_direction, up_scale, up_norm),
        (dilated_direction, dilated_row_scale, dilated_row_norm),
        (paired_direction, pair_scale, pair_norm),
    )
    return (
        upsample_weight,
        dilated_kernel_weight,
        paired_kernel_weight,
        upsample_bias,
        residual_bias,
        weight_rows,
    )


def norm_backward(direction, scale, norm, weight_grad):
    inner = jnp.sum(weight_grad * direction, axis=-1, keepdims=True)
    scale_grad = (inner / norm)[..., 0]
    direction_grad = scale / norm * (weight_grad - inner / (norm * norm) * direction)
    return (direction_grad, scale_grad)


def run_forward(weight_list, first, in_prev, in_next, masks):
    upsample_weight, dilated_kernel_weight, paired_kernel_weight, upsample_bias, residual_bias = (
        weight_list[:5]
    )
    packs, frames = (first.shape[0], first.shape[-1])
    taps_out = jnp.einsum("ik,bit->bkt", upsample_weight, first, preferred_element_type=jnp.float32)
    taps_out = taps_out.reshape(packs, CHANNELS_OUT, KERNEL, frames)
    even_out = taps_out[:, :, 1] + shifted(taps_out[:, :, 3], -1) * in_prev
    odd_out = taps_out[:, :, 2] + shifted(taps_out[:, :, 0], 1) * in_next
    hidden = (
        jnp.stack([even_out, odd_out], axis=-1).reshape(packs, CHANNELS_OUT, 2 * frames)
        + upsample_bias[:, None]
    )
    saved = []
    for block_number in range(RESIDUAL_BLOCKS):
        dilation = 3**block_number
        minus, plus = masks[block_number]
        pre_conv = leaky_smooth(hidden).astype(jnp.bfloat16)
        hidden_low = hidden.astype(jnp.bfloat16)
        stacked_blocks = jnp.concatenate(
            [shifted(pre_conv, -dilation) * minus, pre_conv, shifted(pre_conv, dilation) * plus],
            axis=1,
        )
        dilated_output = (
            jnp.einsum(
                "wd,vdl->vwl",
                dilated_kernel_weight[block_number],
                stacked_blocks,
                preferred_element_type=jnp.float32,
            )
            + residual_bias[block_number, 0][:, None]
        )
        activated = leaky_smooth(dilated_output).astype(jnp.bfloat16)
        branch = jnp.einsum(
            "oi,bit->bot",
            paired_kernel_weight[block_number, 0],
            activated,
            preferred_element_type=jnp.float32,
        )
        shortcut = jnp.einsum(
            "oi,bit->bot",
            paired_kernel_weight[block_number, 1],
            hidden_low,
            preferred_element_type=jnp.float32,
        )
        saved.append((hidden_low, stacked_blocks, dilated_output, activated, hidden))
        hidden = (
            branch
            + shortcut
            + residual_bias[block_number, 1][:, None]
            + residual_bias[block_number, 2][:, None]
        )
    return (hidden, saved)


def per_device(
    signal,
    segments,
    cotangent,
    upsample_direction,
    upsample_gain,
    upsample_bias,
    dilated_direction,
    paired_direction,
    residual_gain,
    residual_bias,
):
    shard_list = (
        upsample_direction,
        upsample_gain,
        upsample_bias,
        dilated_direction,
        paired_direction,
        residual_gain,
        residual_bias,
    )
    frames = signal.shape[-1]
    in_prev = same_seg(segments, -1)[:, None, :]
    in_next = same_seg(segments, 1)[:, None, :]
    seg_out = jnp.repeat(segments, 2, axis=-1)
    masks = []
    for block_number in range(RESIDUAL_BLOCKS):
        dilation = 3**block_number
        masks.append(
            (
                same_seg(seg_out, -dilation)[:, None, :].astype(jnp.bfloat16),
                same_seg(seg_out, dilation)[:, None, :].astype(jnp.bfloat16),
            )
        )
    signal_single = signal.astype(jnp.float32)
    first = leaky_smooth(signal_single).astype(jnp.bfloat16)
    weights_one = prepare(gather_shards(*shard_list))
    final_hidden, unused = run_forward(weights_one, first, in_prev, in_next, masks)
    output = final_hidden.astype(jnp.bfloat16)
    weight_list_two = prepare(gather_shards(*shard_list))
    upsample_weight, dilated_kernel_weight, paired_kernel_weight = (
        weight_list_two[0],
        weight_list_two[1],
        weight_list_two[2],
    )
    unused_final, saved = run_forward(weight_list_two, first, in_prev, in_next, masks)
    grad_hidden = cotangent.astype(jnp.float32)
    pair_grads = [None] * RESIDUAL_BLOCKS
    dilated_gradient_list = [None] * RESIDUAL_BLOCKS
    bias_gradient_list = [None] * RESIDUAL_BLOCKS
    for block_number in reversed(range(RESIDUAL_BLOCKS)):
        dilation = 3**block_number
        minus, plus = masks[block_number]
        hidden_low, stacked_blocks, dilated_output, activated, hidden_in = saved[block_number]
        grad_low = grad_hidden.astype(jnp.bfloat16)
        output_sum = jnp.sum(grad_low.astype(jnp.float32), axis=(0, 2))
        grad_point = jnp.einsum(
            "bot,bit->oi", grad_low, activated, preferred_element_type=jnp.float32
        )
        grad_short = jnp.einsum(
            "bot,bit->oi", grad_low, hidden_low, preferred_element_type=jnp.float32
        )
        activation_gradient = jnp.einsum(
            "oi,bot->bit",
            paired_kernel_weight[block_number, 0],
            grad_low,
            preferred_element_type=jnp.float32,
        )
        dilated_gradient = (activation_gradient * negative_slope(dilated_output)).astype(
            jnp.bfloat16
        )
        dilated_row_sum = jnp.sum(dilated_gradient.astype(jnp.float32), axis=(0, 2))
        dilated_gradient_list[block_number] = jnp.einsum(
            "kjp,khp->jh", dilated_gradient, stacked_blocks, preferred_element_type=jnp.float32
        )
        grad_stack = jnp.einsum(
            "kv,wki->wvi",
            dilated_kernel_weight[block_number],
            dilated_gradient,
            preferred_element_type=jnp.float32,
        )
        grad_pre = (
            grad_stack[:, CHANNELS_OUT : 2 * CHANNELS_OUT]
            + shifted(grad_stack[:, :CHANNELS_OUT] * minus, dilation)
            + shifted(grad_stack[:, 2 * CHANNELS_OUT :] * plus, -dilation)
        )
        grad_hidden = grad_pre * negative_slope(hidden_in) + jnp.einsum(
            "oi,bot->bit",
            paired_kernel_weight[block_number, 1],
            grad_low,
            preferred_element_type=jnp.float32,
        )
        pair_grads[block_number] = jnp.stack([grad_point, grad_short], axis=0)
        bias_gradient_list[block_number] = jnp.stack(
            [dilated_row_sum, output_sum, output_sum], axis=0
        )
    grad_up_low = grad_hidden.astype(jnp.bfloat16)
    up_bias_sum = jnp.sum(grad_up_low.astype(jnp.float32), axis=(0, 2))
    packs = grad_up_low.shape[0]
    paired = grad_up_low.reshape(packs, CHANNELS_OUT, frames, 2)
    even_grad = paired[..., 0]
    odd_grad = paired[..., 1]
    prev_low = in_prev.astype(jnp.bfloat16)
    next_low = in_next.astype(jnp.bfloat16)
    tap_grads = jnp.stack(
        [shifted(odd_grad * next_low, -1), even_grad, odd_grad, shifted(even_grad * prev_low, 1)],
        axis=2,
    )
    tap_grads = tap_grads.reshape(packs, CHANNELS_OUT * KERNEL, frames)
    up_weight_grad = jnp.einsum("bit,bkt->ik", first, tap_grads, preferred_element_type=jnp.float32)
    first_grad = jnp.einsum(
        "ik,bkt->bit", upsample_weight, tap_grads, preferred_element_type=jnp.float32
    )
    signal_grad = (first_grad * negative_slope(signal_single)).astype(jnp.bfloat16)
    weight_rows = weight_list_two[5]
    up_dir_full, up_gain_full = norm_backward(
        weight_rows[0][0], weight_rows[0][1], weight_rows[0][2], up_weight_grad
    )
    dilated_direction_whole, dilated_gain_whole = norm_backward(
        weight_rows[1][0],
        weight_rows[1][1],
        weight_rows[1][2],
        jnp.stack(dilated_gradient_list, axis=0),
    )
    pair_dir_full, paired_gain_whole = norm_backward(
        weight_rows[2][0], weight_rows[2][1], weight_rows[2][2], jnp.stack(pair_grads, axis=0)
    )
    residual_gain_whole = jnp.concatenate(
        [dilated_gain_whole[:, None, :], paired_gain_whole], axis=1
    )
    res_bias_full = jnp.stack(bias_gradient_list, axis=0)
    inner = (
        lax.psum_scatter(
            up_dir_full.astype(jnp.bfloat16), "fsdp", scatter_dimension=1, tiled=True
        ).astype(jnp.float32),
        lax.psum_scatter(
            dilated_direction_whole.astype(jnp.bfloat16), "fsdp", scatter_dimension=2, tiled=True
        ).astype(jnp.float32),
        lax.psum_scatter(
            pair_dir_full.astype(jnp.bfloat16), "fsdp", scatter_dimension=3, tiled=True
        ).astype(jnp.float32),
        lax.psum_scatter(
            up_gain_full.astype(jnp.bfloat16), "fsdp", scatter_dimension=0, tiled=True
        ).astype(jnp.float32),
        lax.psum_scatter(
            up_bias_sum.astype(jnp.bfloat16), "fsdp", scatter_dimension=0, tiled=True
        ).astype(jnp.float32),
        lax.psum_scatter(
            residual_gain_whole.astype(jnp.bfloat16), "fsdp", scatter_dimension=2, tiled=True
        ).astype(jnp.float32),
        lax.psum_scatter(
            res_bias_full.astype(jnp.bfloat16), "fsdp", scatter_dimension=2, tiled=True
        ).astype(jnp.float32),
    )
    directions = (
        lax.psum_scatter(inner[0], "dp", scatter_dimension=0, tiled=True),
        lax.psum_scatter(inner[1], "dp", scatter_dimension=1, tiled=True),
        lax.psum_scatter(inner[2], "dp", scatter_dimension=2, tiled=True),
    )
    smalls = lax.psum((inner[3], inner[4], inner[5], inner[6]), "dp")
    return (
        output,
        signal_grad,
        directions[0],
        smalls[0],
        smalls[1],
        directions[1],
        directions[2],
        smalls[2],
        smalls[3],
    )


def solution(mesh):
    return jax.shard_map(
        per_device,
        mesh=mesh,
        in_specs=(
            P(("dp", "fsdp"), None, None),
            P(("dp", "fsdp"), None),
            P(("dp", "fsdp"), None, None),
            P("dp", "fsdp"),
            P("fsdp"),
            P("fsdp"),
            P(None, "dp", "fsdp"),
            P(None, None, "dp", "fsdp"),
            P(None, None, "fsdp"),
            P(None, None, "fsdp"),
        ),
        out_specs=(
            P(("dp", "fsdp"), None, None),
            P(("dp", "fsdp"), None, None),
            P("dp", "fsdp"),
            P("fsdp"),
            P("fsdp"),
            P(None, "dp", "fsdp"),
            P(None, None, "dp", "fsdp"),
            P(None, None, "fsdp"),
            P(None, None, "fsdp"),
        ),
        check_vma=False,
    )
```

profile of v0, /device:TPU:0, one launch (start us, length us, event | category | flops | bytes accessed | tf_op | source)
XLA Modules:
  0.0 943.0 jit_solution(12643552015424759688)
XLA Ops:
  17.3 32.2 %all_gather.44 = bf16[3,3,32]{1,0,2:T(4,128)(2,1)S(1)} all-gather(bf16[3,3,4]{1,0,2:T(4,128)(2,1)S(1)} %copy.333), channel_id=1, replica_groups=mesh['dp'=4,'fsdp'=8] {'fsdp'}, dimensions={2}, use_global_device_ids=true | all-gather | bytes 648 | tf_op jit(solution)/shard_map/all_gather | solution.py:48
  50.1 21.3 %all-reduce.36 = (bf16[32]{0:T(256)(128)(2,1)S(1)}, bf16[64]{0:T(256)(128)(2,1)S(1)}) all-reduce(bf16[32]{0:T(256)(128)(2,1)S(1)} %dynamic-update-slice.1, bf16[64]{0:T(256)(128)(2,1)S(1)} %dynamic-update-slice), channel_id=1, replica_groups=mesh['dp'=4,'fsdp'=8] {'fsdp'}, use_global_device_ids=true, to_apply=%add.25 | all-reduce | flops 96 | bytes 384
  71.8 30.4 %all_gather.47 = bf16[3,3,32]{1,0,2:T(4,128)(2,1)S(1)} all-gather(bf16[3,3,4]{1,0,2:T(4,128)(2,1)S(1)} %copy.337), channel_id=1, replica_groups=mesh['dp'=4,'fsdp'=8] {'fsdp'}, dimensions={2}, use_global_device_ids=true | all-gather | bytes 648 | tf_op jit(solution)/shard_map/all_gather | solution.py:49
  102.3 30.4 %all_gather.41 = bf16[16,128]{0,1:T(8,128)(2,1)S(1)} all-gather(bf16[16,16]{0,1:T(8,128)(2,1)S(1)} %copy.320), channel_id=1, replica_groups=mesh['dp'=4,'fsdp'=8] {'fsdp'}, dimensions={1}, use_global_device_ids=true | all-gather | bytes 4608 | tf_op jit(solution)/shard_map/all_gather | solution.py:43
  132.7 5.2 all_gather.42
  139.5 30.7 %all_gather.48 = bf16[3,2,8,32]{2,1,0,3:T(2,128)(2,1)S(1)} all-gather(bf16[3,2,8,4]{2,1,0,3:T(2,128)(2,1)S(1)} %copy.338), channel_id=1, replica_groups=mesh['dp'=4,'fsdp'=8] {'fsdp'}, dimensions={3}, use_global_device_ids=true | all-gather | bytes 3456 | tf_op jit(solution)/shard_map/all_gather | solution.py:45
  170.2 5.2 all_gather.49
  176.1 30.5 %all_gather.45 = bf16[3,8,96]{1,0,2:T(4,128)(2,1)S(1)} all-gather(bf16[3,8,12]{1,0,2:T(4,128)(2,1)S(1)} %copy.335), channel_id=1, replica_groups=mesh['dp'=4,'fsdp'=8] {'fsdp'}, dimensions={2}, use_global_device_ids=true | all-gather | bytes 5184 | tf_op jit(solution)/shard_map/all_gather | solution.py:44
  206.8 5.2 all_gather.46
  220.4 11.1 %convolution_bitcast_fusion.9 = f32[8,128,4096]{2,1,0:T(8,128)} fusion(bf16[64,128]{1,0:T(8,128)(2,1)S(1)} %all_gather.42, f32[64]{0:T(128)S(1)} %sqrt.49, f32[64]{0:T(128)S(1)} %convert_element_type.259, bf16[8,64,4096]{2,1,0:T(8,128)(2,1)} %param.10), kind=kOutput, calls=%fused_computation.49 | convolution fusion | flops 555778048 | bytes 20988416 | tf_op jit(solution)/shard_map/ik,bit->bkt/dot_general | solution.py:109
  231.5 19.0 %reshape.161 = f32[8,32,4,4096]{3,2,1,0:T(4,128)} reshape(f32[8,128,4096]{2,1,0:T(8,128)} %convolution_bitcast_fusion.9) | data formatting | bytes 33554432 | tf_op jit(solution)/shard_map/reshape | solution.py:110
  250.5 38.7 %fusion.113 = (f32[8,32,1,4096]{3,2,1,0:T(1,128)}, f32[8,32,1,4096]{3,2,1,0:T(1,128)}, f32[8,32,1,4096]{3,2,1,0:T(1,128)}, f32[8,32,1,4096]{3,2,1,0:T(1,128)}) fusion(f32[8,32,4,4096]{3,2,1,0:T(4,128)} %reshape.161), kind=kLoop, calls=%fused_computation.248 | loop fusion | bytes 33554432 | tf_op jit(solution)/shard_map/slice | solution.py:111
  289.1 11.6 %copy_bitcast_fusion = (f32[8,32,4096]{2,1,0:T(8,128)S(1)}, f32[8,32,4096]{2,1,0:T(8,128)S(1)}) fusion(f32[8,32,1,4096]{3,2,1,0:T(1,128)} %get-tuple-element.112, f32[8,32,1,4096]{3,2,1,0:T(1,128)} %get-tuple-element.109), kind=kLoop, calls=%fused_computation.105 | loop fusion | bytes 16777216 | tf_op jit(solution)/shard_map/squeeze | solution.py:112
  302.9 4.4 fusion.49
  307.3 4.4 fusion.51
  311.7 5.3 pad_maximum_fusion.4
  317.0 18.1 %copy.340 = bf16[8,32,4096,2]{1,0,3,2:T(8,128)(2,1)} copy(bf16[8,32,4096,2]{2,1,3,0:T(8,128)(2,1)} %get-tuple-element.114) | data formatting | bytes 8388608 | tf_op jit(solution)/shard_map/convert_element_type | solution.py:122
  335.1 23.2 %copy.326 = f32[8,32,4096,2]{1,0,3,2:T(8,128)} copy(f32[8,32,4096,2]{2,1,3,0:T(8,128)} %get-tuple-element.113) | data formatting | bytes 16777216 | tf_op jit(solution)/shard_map/stack | solution.py:114
  358.3 21.7 %copy.327 = f32[8,32,8192]{2,1,0:T(8,128)} copy(f32[8,32,8192]{1,0,2:T(8,128)} %bitcast.277) | data formatting | bytes 16777216 | tf_op jit(solution)/shard_map/reshape | solution.py:114
  380.0 5.0 add_convert_fusion.6
  387.1 4.7 pad_multiply_fusion.5
  395.1 14.7 %fusion = f32[8,8192,32]{1,2,0:T(8,128)} fusion(bf16[8,32,8192]{1,0,2:T(8,128)(2,1)} %bitcast.283, bf16[3,2,32,32]{3,2,1,0:T(8,128)(2,1)S(1)} %fusion.72), kind=kOutput, calls=%fused_computation.1 | convolution fusion | flops 134217728 | bytes 12591104 | tf_op jit(solution)/shard_map/oi,bit->bot/dot_general | solution.py:143
  409.8 8.1 fusion.12
  419.7 11.2 %add_convert_fusion.3 = (bf16[8,32,8192]{2,1,0:T(8,128)(2,1)S(1)}, f32[8,32,8192]{2,1,0:T(8,128)}) fusion(f32[32]{0:T(128)S(1)} %get-tuple-element.78, f32[32]{0:T(128)S(1)} %get-tuple-element.79, f32[8,8192,32]{1,2,0:T(8,128)S(1)} %copy-done.19, f32[8,32,8192]{2,1,0:T(8,128)} %fusion.12, bf16[3,2,32,32]{3,2,1,0:T(8,128)(2,1)S(1)} %fusion.72), kind=kOutput, calls=%fused_computation.81 | convolution fusion | flops 174063616 | bytes 29369344 | tf_op jit(solution)/shard_map/oi,bit->bot/dot_general | solution.py:137
  438.6 8.1 add_convert_fusion.2
  448.7 9.0 add_convert_fusion.1
  459.8 4.7 pad_multiply_fusion.1
  467.5 9.7 %add_convert_fusion = (bf16[8,32,8192]{2,1,0:T(8,128)(2,1)}, f32[8,32,8192]{2,1,0:T(8,128)}) fusion(f32[32]{0:T(128)S(1)} %copy-done.66, bf16[8,32,8192]{2,1,0:T(8,128)(2,1)} %pad_multiply_fusion, bf16[8,32,8192]{2,1,0:T(8,128)(2,1)S(1)} %get-tuple-element.152, bf16[8,32,8192]{2,1,0:T(8,128)(2,1)} %pad_multiply_fusion.1, bf16[3,32,96]{2,1,0:T(8,128)(2,1)S(1)} %fusion.79), kind=kOutput, calls=%fused_computation.75 | convolution fusion | flops 459276288 | bytes 25174528 | tf_op jit(solution)/shard_map/wd,vdl->vwl/dot_general | solution.py:128
  477.3 8.0 fusion.123
  487.3 10.1 %convolution_bitcast_fusion.2 = f32[8,96,8192]{2,1,0:T(8,128)} fusion(bf16[8,32,8192]{2,1,0:T(8,128)(2,1)S(1)} %get-tuple-element.161, bf16[3,32,96]{2,1,0:T(8,128)(2,1)S(1)} %fusion.79), kind=kOutput, calls=%fused_computation.5 | convolution fusion | flops 402653184 | bytes 29368320 | tf_op jit(solution)/shard_map/kv,wki->wvi/dot_general | solution.py:234
  497.4 10.2 %fusion.112 = (f32[8,32,8192]{2,1,0:T(8,128)}, f32[8,32,8192]{2,1,0:T(8,128)S(1)}) fusion(f32[8,96,8192]{2,1,0:T(8,128)} %convolution_bitcast_fusion.2), kind=kLoop, calls=%fused_computation.247 | loop fusion | bytes 33554432 | tf_op jit(solution)/shard_map/slice | solution.py:242
  507.7 9.0 slice_multiply_fusion.5
  520.8 14.0 %fusion.124 = (bf16[32]{0:T(256)(128)(2,1)}, bf16[8,32,8192]{2,1,0:T(8,128)(2,1)S(1)}) fusion(bf16[8,32,8192]{2,1,0:T(8,128)(2,1)S(1)} %copy-done, bf16[3,2,32,32]{3,2,1,0:T(8,128)(2,1)} %copy-done.43, f32[8,32,8192]{2,1,0:T(8,128)} %get-tuple-element.153, f32[8,32,8183]{2,1,0:T(8,128)} %slice_multiply_fusion.4, f32[8,32,8183]{2,1,0:T(8,128)} %slice_multiply_fusion.5, ...), kind=kOutput, calls=%fused_computation.259 | convolution fusion | flops 165674976 | bytes 41951296 | tf_op jit(solution)/shard_map/oi,bot->bit/dot_general | solution.py:245
  534.8 9.2 fusion.125
  545.9 10.2 %convolution_bitcast_fusion.1 = f32[8,96,8192]{2,1,0:T(8,128)} fusion(bf16[8,32,8192]{2,1,0:T(8,128)(2,1)S(1)} %get-tuple-element.165, bf16[3,32,96]{2,1,0:T(8,128)(2,1)S(1)} %fusion.79), kind=kOutput, calls=%fused_computation.4 | convolution fusion | flops 402653184 | bytes 29368320 | tf_op jit(solution)/shard_map/kv,wki->wvi/dot_general | solution.py:234
  556.1 6.5 fusion.111
  562.6 6.4 slice_multiply_fusion.3
  569.1 5.0 slice_multiply_fusion.2
  574.1 14.4 %fusion.126 = (bf16[32]{0:T(256)(128)(2,1)}, bf16[8,32,8192]{2,1,0:T(8,128)(2,1)S(1)}) fusion(bf16[8,32,8192]{2,1,0:T(8,128)(2,1)S(1)} %get-tuple-element.163, bf16[3,2,32,32]{3,2,1,0:T(8,128)(2,1)} %copy-done.43, f32[8,32,8192]{2,1,0:T(8,128)} %get-tuple-element.149, f32[8,32,8189]{2,1,0:T(8,128)} %slice_multiply_fusion.2, ...), kind=kOutput, calls=%fused_computation.261 | convolution fusion | flops 165674976 | bytes 41951296 | tf_op jit(solution)/shard_map/oi,bot->bit/dot_general | solution.py:245
  588.5 9.1 fusion.127
  599.6 10.2 %convolution_bitcast_fusion = f32[8,96,8192]{2,1,0:T(8,128)} fusion(bf16[8,32,8192]{2,1,0:T(8,128)(2,1)S(1)} %get-tuple-element.169, bf16[3,32,96]{2,1,0:T(8,128)(2,1)S(1)} %fusion.79), kind=kOutput, calls=%fused_computation.3 | convolution fusion | flops 402653184 | bytes 29368320 | tf_op jit(solution)/shard_map/kv,wki->wvi/dot_general | solution.py:234
  609.8 10.0 %fusion.110 = (f32[8,32,8192]{2,1,0:T(8,128)}, f32[8,32,8192]{2,1,0:T(8,128)S(1)}) fusion(f32[8,96,8192]{2,1,0:T(8,128)} %convolution_bitcast_fusion), kind=kLoop, calls=%fused_computation.245 | loop fusion | bytes 33554432 | tf_op jit(solution)/shard_map/slice | solution.py:242
  619.8 9.0 slice_multiply_fusion.1
  633.0 15.4 %fusion.122 = (bf16[32]{0:T(256)(128)(2,1)}, bf16[8,32,8192]{2,1,0:T(8,128)(2,1)}) fusion(bf16[8,32,8192]{2,1,0:T(8,128)(2,1)} %copy-done.20, bf16[3,2,32,32]{3,2,1,0:T(8,128)(2,1)S(1)} %copy-done.44, f32[8,32,8192]{2,1,0:T(8,128)S(1)} %bitcast.279, f32[32]{0:T(128)S(1)} %copy-done.56, f32[8,32,8191]{2,1,0:T(8,128)} %slice_multiply_fusion, ...), kind=kOutput, calls=%fused_computation.257 | convolution fusion | flops 167772128 | bytes 41949760 | tf_op jit(solution)/shard_map/oi,bot->bit/dot_general | solution.py:245
  648.4 16.8 %copy.356 = bf16[8,32,8192]{1,0,2:T(8,128)(2,1)} copy(bf16[8,32,8192]{2,1,0:T(8,128)(2,1)} %get-tuple-element.159) | data formatting | bytes 8388608 | tf_op jit(solution)/shard_map/convert_element_type | solution.py:255
  665.2 12.9 %slice_bitcast_fusion.3 = (bf16[8,32,4096]{1,0,2:T(8,128)(2,1)S(1)}, bf16[8,32,1,4096]{1,0,3,2:T(8,128)(2,1)}, bf16[8,32,4096]{1,0,2:T(8,128)(2,1)S(1)}, bf16[8,32,1,4096]{1,0,3,2:T(8,128)(2,1)}) fusion(bf16[8,32,4096,2]{1,0,3,2:T(8,128)(2,1)} %bitcast.282), kind=kLoop, calls=%fused_computation.93 | loop fusion | bytes 12582912 | tf_op jit(solution)/shard_map/squeeze | solution.py:260
  678.2 11.8 %slice_multiply_fusion.7 = bf16[8,32,4095]{1,0,2:T(8,128)(2,1)S(1)} fusion(bf16[8,32,4096]{1,0,2:T(8,128)(2,1)S(1)} %get-tuple-element.105, bf16[8,4095]{0,1:T(8,128)(2,1)S(1)} %copy-done.25), kind=kLoop, calls=%fused_computation.89 | loop fusion | flops 1048320 | bytes 4258800 | tf_op jit(solution)/shard_map/mul | solution.py:264
  694.2 11.8 %slice_multiply_fusion.6 = bf16[8,32,4095]{1,0,2:T(8,128)(2,1)S(1)} fusion(bf16[8,32,4096]{1,0,2:T(8,128)(2,1)S(1)} %get-tuple-element.107, bf16[8,4095]{0,1:T(8,128)(2,1)S(1)} %copy-done.24), kind=kLoop, calls=%fused_computation.88 | loop fusion | flops 1048320 | bytes 4258800 | tf_op jit(solution)/shard_map/mul | solution.py:264
  706.0 4.3 pad_bitcast_fusion
  710.3 23.1 %pad_maximum_fusion = bf16[8,32,4,4096]{1,0,3,2:T(8,128)(2,1)} fusion(bf16[8,32,1,4096]{1,0,3,2:T(8,128)(2,1)} %pad_bitcast_fusion, bf16[8,32,1,4096]{1,0,3,2:T(8,128)(2,1)} %get-tuple-element.106, bf16[8,32,1,4096]{1,0,3,2:T(8,128)(2,1)} %get-tuple-element.108, bf16[8,32,1,4096]{1,0,3,2:T(8,128)(2,1)} %pad_bitcast_fusion.1), kind=kLoop, calls=%fused_computation | loop fusion | flops 12582912 | bytes 16777216 | tf_op jit(solution)/shard_map/stack | solution.py:263
  733.4 35.8 %copy.363 = bf16[8,32,4,4096]{3,2,1,0:T(4,128)(2,1)} copy(bf16[8,32,4,4096]{1,0,3,2:T(8,128)(2,1)} %pad_maximum_fusion) | data formatting | bytes 16777216 | tf_op jit(solution)/shard_map/stack | solution.py:263
  769.2 12.5 %reshape.164 = bf16[8,128,4096]{2,1,0:T(8,128)(2,1)} reshape(bf16[8,32,4,4096]{3,2,1,0:T(4,128)(2,1)} %copy.363) | data formatting | bytes 16777216 | tf_op jit(solution)/shard_map/reshape | solution.py:267
  781.7 7.9 fusion.88
  793.5 6.0 fusion.62
  799.5 7.9 fusion.68
  808.7 5.5 fusion.95
  816.4 7.7 fusion.67
  824.2 6.0 fusion.59
  837.5 6.2 fusion.66
  843.8 11.7 %fusion.38 = bf16[8,64,4096]{2,1,0:T(8,128)(2,1)} fusion(bf16[8,128,4096]{2,1,0:T(8,128)(2,1)} %reshape.164, bf16[8,64,4096]{2,1,0:T(8,128)(2,1)} %param.10, bf16[64,128]{1,0:T(8,128)(2,1)S(1)} %copy-done.42, f32[64]{0:T(128)S(1)} %copy-done.83, f32[64]{0:T(128)S(1)} %copy-done.81), kind=kOutput, calls=%fused_computation.72 | convolution fusion | flops 562069504 | bytes 16794112 | tf_op jit(solution)/shard_map/ik,bkt->bit/dot_general | solution.py:269
  858.9 34.7 %all-reduce.35 = (bf16[64]{0:T(256)(128)(2,1)S(1)}, bf16[32]{0:T(256)(128)(2,1)S(1)}, bf16[3,32,96]{1,0,2:T(4,128)(2,1)S(1)}, bf16[3,2,32,32]{2,1,0,3:T(2,128)(2...) all-reduce(bf16[64]{0:T(256)(128)(2,1)S(1)} %get-tuple-element.143,, ...), channel_id=4, replica_groups=mesh['dp'=4,'fsdp'=8] {'fsdp'}, use_global_device_ids=true, to_apply=%region_6.7.clone | all-reduce | flops 16032 | bytes 64128
  894.0 9.1 fusion.26
  903.8 11.6 %all-reduce.34 = (f32[8]{0:T(128)}, f32[4]{0:T(128)}, f32[3,32,12]{2,0,1:T(4,128)S(1)}, f32[3,2,32,4]{2,1,0,3:T(2,128)S(1)}, f32[3,3,4]{2,1,0:T(4,128)}, /*index=5*/f32[3,3,4]{2,1,0:T(4,128)}) all-reduce(f32[8]{0:T(128)S(1)} %dynamic-slice_convert_fusion.4, ...), channel_id=1, replica_groups=mesh['dp'=4,'fsdp'=8] {'dp'}, use_global_device_ids=true, to_apply=%region_7.8 | all-reduce | flops 2004 | bytes 16032 | tf_op jit(solution)/shard_map/psum | solution.py:318
  918.1 17.6 %reduce-scatter.8.cloned.1.call-done = f32[16,16]{1,0:T(8,128)} async-done(((f32[64,16]{1,0:T(8,128)}), f32[16,16]{1,0:T(8,128)}) %reduce-scatter.8.cloned.1.call-update) | async-done | bytes 1040 | tf_op jit(solution)/shard_map/reduce_scatter | solution.py:314
  (289 shorter events, 81.9 us)
Async XLA Ops:
  7.2 908.2 %reduce-scatter.10.cloned.1.call-start = ((), (), s32[]{:S(2)}) async-start(), calls=%async_computation.3 | async-start | bytes 36864
  8.2 7.1 copy-start.62
  8.2 9.0 copy-start.58
  8.2 41.5 %copy-start.77 = (bf16[4]{0:T(256)(128)(2,1)S(1)}, bf16[4]{0:T(256)(128)(2,1)}, u32[]{:S(2)}) copy-start(bf16[4]{0:T(256)(128)(2,1)} %param.15) | copy-start | bytes 28
  8.2 41.7 %copy-start.78 = (bf16[8]{0:T(256)(128)(2,1)S(1)}, bf16[8]{0:T(256)(128)(2,1)}, u32[]{:S(2)}) copy-start(bf16[8]{0:T(256)(128)(2,1)} %param.14) | copy-start | bytes 52
  8.2 63.3 %copy-start.57 = (bf16[16,16]{1,0:T(8,128)(2,1)S(1)}, bf16[16,16]{1,0:T(8,128)(2,1)}, u32[]{:S(2)}) copy-start(bf16[16,16]{1,0:T(8,128)(2,1)} %param.13) | copy-start | bytes 1540
  8.2 63.4 %copy-start.59 = (bf16[3,3,4]{2,1,0:T(4,128)(2,1)S(1)}, bf16[3,3,4]{2,1,0:T(4,128)(2,1)}, u32[]{:S(2)}) copy-start(bf16[3,3,4]{2,1,0:T(4,128)(2,1)} %param.19) | copy-start | bytes 220
  8.2 63.5 %copy-start.53 = (bf16[3,2,8,4]{2,3,1,0:T(4,128)(2,1)S(1)}, bf16[3,2,8,4]{2,3,1,0:T(4,128)(2,1)}, u32[]{:S(2)}) copy-start(bf16[3,2,8,4]{2,3,1,0:T(4,128)(2,1)} %param.17) | copy-start | bytes 1156
  8.2 63.5 %copy-start.54 = (bf16[3,8,12]{2,1,0:T(8,128)(2,1)S(1)}, bf16[3,8,12]{2,1,0:T(8,128)(2,1)}, u32[]{:S(2)}) copy-start(bf16[3,8,12]{2,1,0:T(8,128)(2,1)} %param.16) | copy-start | bytes 1732
  8.4 204.3 %copy-start.40 = (s32[8,4096]{1,0:T(8,128)S(1)}, s32[8,4096]{1,0:T(8,128)}, u32[]{:S(2)}) copy-start(s32[8,4096]{1,0:T(8,128)} %param.11) | copy-start | bytes 393220
  49.6 88.5 %copy-start.45 = (bf16[3,3,32]{2,1,0:T(4,128)(2,1)}, bf16[3,3,32]{2,1,0:T(4,128)(2,1)S(1)}, u32[]{:S(2)}) copy-start(bf16[3,3,32]{2,1,0:T(4,128)(2,1)S(1)} %copy.334) | copy-start | bytes 1732
  49.6 88.5 %copy-start.51 = (f32[3,1,32]{2,1,0:T(1,128)}, f32[3,1,32]{2,1,0:T(1,128)S(1)}, u32[]{:S(2)}) copy-start(f32[3,1,32]{2,1,0:T(1,128)S(1)} %slice.275) | copy-start | bytes 1156
  71.5 140.5 %copy-start.70 = (bf16[64]{0:T(256)(128)(2,1)}, bf16[64]{0:T(256)(128)(2,1)S(1)}, u32[]{:S(2)}) copy-start(bf16[64]{0:T(256)(128)(2,1)S(1)} %get-tuple-element.94) | copy-start | bytes 388
  71.5 308.6 %copy-start.55 = (f32[32]{0:T(128)}, f32[32]{0:T(128)S(1)}, u32[]{:S(2)}) copy-start(f32[32]{0:T(128)S(1)} %convert_element_type.264) | copy-start | bytes 388
  71.5 160.0 %copy-start.80 = (f32[64]{0:T(128)}, f32[64]{0:T(128)S(1)}, u32[]{:S(2)}) copy-start(f32[64]{0:T(128)S(1)} %convert_element_type.259) | copy-start | bytes 772
  137.9 93.6 %copy-start.41 = (bf16[64,128]{1,0:T(8,128)(2,1)}, bf16[64,128]{1,0:T(8,128)(2,1)S(1)}, u32[]{:S(2)}) copy-start(bf16[64,128]{1,0:T(8,128)(2,1)S(1)} %all_gather.42) | copy-start | bytes 49156
  138.0 37.4 %copy-start.63 = (f32[64]{0:T(128)}, f32[64]{0:T(128)S(1)}, u32[]{:S(2)}) copy-start(f32[64]{0:T(128)S(1)} %fusion.87) | copy-start | bytes 772
  138.0 93.5 %copy-start.82 = (f32[64]{0:T(128)}, f32[64]{0:T(128)S(1)}, u32[]{:S(2)}) copy-start(f32[64]{0:T(128)S(1)} %sqrt.49) | copy-start | bytes 772
  175.4 219.4 %copy-start.32 = (bf16[3,2,32,32]{3,2,1,0:T(8,128)(2,1)}, bf16[3,2,32,32]{3,2,1,0:T(8,128)(2,1)S(1)}, u32[]{:S(2)}) copy-start(bf16[3,2,32,32]{3,2,1,0:T(8,128)(2,1)S(1)} %all_gather.49) | copy-start | bytes 36868
  211.9 183.0 %copy-start.38 = (bf16[3,32,96]{2,1,0:T(8,128)(2,1)}, bf16[3,32,96]{2,1,0:T(8,128)(2,1)S(1)}, u32[]{:S(2)}) copy-start(bf16[3,32,96]{2,1,0:T(8,128)(2,1)S(1)} %all_gather.46) | copy-start | bytes 55300
  395.0 82.3 %copy-start.43 = (bf16[3,2,32,32]{3,2,1,0:T(8,128)(2,1)}, bf16[3,2,32,32]{3,2,1,0:T(8,128)(2,1)S(1)}, u32[]{:S(2)}) copy-start(bf16[3,2,32,32]{3,2,1,0:T(8,128)(2,1)S(1)} %fusion.72) | copy-start | bytes 36868
  409.8 10.0 %copy-start.19 = (f32[8,8192,32]{1,2,0:T(8,128)S(1)}, f32[8,8192,32]{1,2,0:T(8,128)}, u32[]{:S(2)}) copy-start(f32[8,8192,32]{1,2,0:T(8,128)} %fusion) | copy-start | bytes 25165828
  430.9 7.7 copy-start.5
  435.4 11.4 %copy-start.23 = (bf16[8,32,8192]{2,1,0:T(8,128)(2,1)}, bf16[8,32,8192]{2,1,0:T(8,128)(2,1)S(1)}, u32[]{:S(2)}) copy-start(bf16[8,32,8192]{2,1,0:T(8,128)(2,1)S(1)} %pad_multiply_fusion.3) | copy-start | bytes 12582916
  457.8 9.8 %copy-start.7 = (bf16[8,32,8192]{2,1,0:T(8,128)(2,1)}, bf16[8,32,8192]{2,1,0:T(8,128)(2,1)S(1)}, u32[]{:S(2)}) copy-start(bf16[8,32,8192]{2,1,0:T(8,128)(2,1)S(1)} %get-tuple-element.152) | copy-start | bytes 12582916
  459.8 7.8 copy-start.66
  467.5 9.7 %copy-start = (bf16[8,32,8192]{2,1,0:T(8,128)(2,1)S(1)}, bf16[8,32,8192]{2,1,0:T(8,128)(2,1)}, u32[]{:S(2)}) copy-start(bf16[8,32,8192]{2,1,0:T(8,128)(2,1)} %param.12) | copy-start | bytes 12582916
  497.4 10.2 %copy-start.37 = (f32[8,8183]{1,0:T(8,128)S(1)}, f32[8,8183]{1,0:T(8,128)}, u32[]{:S(2)}) copy-start(f32[8,8183]{1,0:T(8,128)} %slice.316) | copy-start | bytes 785572
  507.7 9.0 copy-start.36
  534.8 39.3 %copy-start.9 = (bf16[8,32,8192]{2,1,0:T(8,128)(2,1)}, bf16[8,32,8192]{2,1,0:T(8,128)(2,1)S(1)}, u32[]{:S(2)}) copy-start(bf16[8,32,8192]{2,1,0:T(8,128)(2,1)S(1)} %get-tuple-element.163) | copy-start | bytes 12582916
  588.5 9.1 copy-start.20
  609.8 10.1 %copy-start.35 = (f32[8,8191]{1,0:T(8,128)S(1)}, f32[8,8191]{1,0:T(8,128)}, u32[]{:S(2)}) copy-start(f32[8,8191]{1,0:T(8,128)} %slice.330) | copy-start | bytes 786340
  619.8 9.0 copy-start.34
  619.8 13.2 %slice-start = ((s8[8388608]{0:T(1024)(128)(4,1)}), s8[4194304]{0:T(1024)(128)(4,1)S(1)}, s32[]{:S(2)}) async-start(s8[8388608]{0:T(1024)(128)(4,1)} %bitcast.278), calls=%async_computation.4 | async-start | bytes 8388608
  665.2 12.9 %copy-start.25 = (bf16[8,4095]{0,1:T(8,128)(2,1)S(1)}, bf16[8,4095]{0,1:T(8,128)(2,1)}, u32[]{:S(2)}) copy-start(bf16[8,4095]{0,1:T(8,128)(2,1)} %copy.435) | copy-start | bytes 196564
  769.2 12.6 %copy-start.42 = (bf16[64,128]{1,0:T(8,128)(2,1)S(1)}, bf16[64,128]{1,0:T(8,128)(2,1)}, u32[]{:S(2)}) copy-start(bf16[64,128]{1,0:T(8,128)(2,1)} %copy-done.41) | copy-start | bytes 49156
  781.7 8.0 copy-start.64
  781.7 8.0 copy-start.71
  781.7 11.7 %copy-start.46 = (bf16[3,3,32]{2,1,0:T(4,128)(2,1)S(1)}, bf16[3,3,32]{2,1,0:T(4,128)(2,1)}, u32[]{:S(2)}) copy-start(bf16[3,3,32]{2,1,0:T(4,128)(2,1)} %copy-done.45) | copy-start | bytes 1732
  790.6 145.1 %reduce-scatter.8.cloned.1.call-start = ((), (), s32[]{:S(2)}) async-start(), calls=%async_computation.2 | async-start | bytes 40960 | tf_op jit(solution)/shard_map/reduce_scatter | solution.py:314
  799.5 8.0 copy-start.1
  799.5 8.0 copy-start.4
  808.7 6.5 copy-start.12
  808.7 7.7 copy-start.6
  815.2 15.0 %slice-start.2 = ((s8[8388608]{0:T(1024)(128)(4,1)}), s8[4194304]{0:T(1024)(128)(4,1)S(1)}, s32[]{:S(2)}) async-start(s8[8388608]{0:T(1024)(128)(4,1)} %bitcast.280), calls=%async_computation.6 | async-start | bytes 8388608
  816.4 13.8 %slice-start.3 = ((s8[8388608]{0:T(1024)(128)(4,1)}), s8[4194304]{0:T(1024)(128)(4,1)S(1)}, s32[]{:S(2)}) async-start(s8[8388608]{0:T(1024)(128)(4,1)} %bitcast.280), calls=%async_computation.7 | async-start | bytes 8388608
  824.2 6.1 copy-start.21
  824.2 7.6 slice-start.4
  837.5 6.2 copy-start.81
  837.5 6.2 copy-start.83
  843.7 11.8 %copy-start.79 = (u32[32]{0:T(128)S(1)}, u32[32]{0:T(128)}, u32[]{:S(2)}) copy-start(u32[32]{0:T(128)} %constant.129) | copy-start | bytes 388
  843.7 14.2 %copy-start.39 = (bf16[3,32,96]{2,1,0:T(8,128)(2,1)S(1)}, bf16[3,32,96]{2,1,0:T(8,128)(2,1)}, u32[]{:S(2)}) copy-start(bf16[3,32,96]{2,1,0:T(8,128)(2,1)} %copy-done.38) | copy-start | bytes 55300
  843.7 14.3 %copy-start.50 = (f32[3,32]{1,0:T(4,128)S(1)}, f32[3,32]{1,0:T(4,128)}, u32[]{:S(2)}) copy-start(f32[3,32]{1,0:T(4,128)} %copy-done.49) | copy-start | bytes 1156
  843.7 14.3 %copy-start.52 = (f32[3,1,32]{2,1,0:T(1,128)S(1)}, f32[3,1,32]{2,1,0:T(1,128)}, u32[]{:S(2)}) copy-start(f32[3,1,32]{2,1,0:T(1,128)} %copy-done.51) | copy-start | bytes 1156
  843.7 14.4 %copy-start.33 = (bf16[3,2,32,32]{3,2,1,0:T(8,128)(2,1)S(1)}, bf16[3,2,32,32]{3,2,1,0:T(8,128)(2,1)}, u32[]{:S(2)}) copy-start(bf16[3,2,32,32]{3,2,1,0:T(8,128)(2,1)} %copy-done.32) | copy-start | bytes 36868
  843.7 14.5 %copy-start.48 = (f32[3,2,32]{2,1,0:T(2,128)S(1)}, f32[3,2,32]{2,1,0:T(2,128)}, u32[]{:S(2)}) copy-start(f32[3,2,32]{2,1,0:T(2,128)} %copy-done.47) | copy-start | bytes 2308
  843.7 15.0 %copy-start.72 = (bf16[32]{0:T(256)(128)(2,1)S(1)}, bf16[32]{0:T(256)(128)(2,1)}, u32[]{:S(2)}) copy-start(bf16[32]{0:T(256)(128)(2,1)} %get-tuple-element.160) | copy-start | bytes 196
  843.8 15.0 %copy-start.73 = (bf16[32]{0:T(256)(128)(2,1)S(1)}, bf16[32]{0:T(256)(128)(2,1)}, u32[]{:S(2)}) copy-start(bf16[32]{0:T(256)(128)(2,1)} %get-tuple-element.162) | copy-start | bytes 196
  843.8 15.0 %copy-start.74 = (bf16[32]{0:T(256)(128)(2,1)S(1)}, bf16[32]{0:T(256)(128)(2,1)}, u32[]{:S(2)}) copy-start(bf16[32]{0:T(256)(128)(2,1)} %get-tuple-element.164) | copy-start | bytes 196
  843.8 15.0 %copy-start.75 = (bf16[32]{0:T(256)(128)(2,1)S(1)}, bf16[32]{0:T(256)(128)(2,1)}, u32[]{:S(2)}) copy-start(bf16[32]{0:T(256)(128)(2,1)} %get-tuple-element.166) | copy-start | bytes 196
  843.8 15.0 %copy-start.76 = (bf16[32]{0:T(256)(128)(2,1)S(1)}, bf16[32]{0:T(256)(128)(2,1)}, u32[]{:S(2)}) copy-start(bf16[32]{0:T(256)(128)(2,1)} %get-tuple-element.168) | copy-start | bytes 196
  843.8 15.1 %copy-start.65 = (bf16[32]{0:T(256)(128)(2,1)S(1)}, bf16[32]{0:T(256)(128)(2,1)}, u32[]{:S(2)}) copy-start(bf16[32]{0:T(256)(128)(2,1)} %get-tuple-element.158) | copy-start | bytes 196
  843.8 50.2 %copy-start.60 = (f32[32]{0:T(128)S(1)}, f32[32]{0:T(128)}, u32[]{:S(2)}) copy-start(f32[32]{0:T(128)} %get-tuple-element.72) | copy-start | bytes 388
  843.8 50.2 %copy-start.61 = (f32[32]{0:T(128)S(1)}, f32[32]{0:T(128)}, u32[]{:S(2)}) copy-start(f32[32]{0:T(128)} %get-tuple-element.73) | copy-start | bytes 388
  (28 other events, 83.9 us)
Sparse Core Ops, SparseCore 0:
  790.7 50.8 reduce-scatter.9
  916.9 18.7 reduce-scatter.7
where the time goes:
time: 955 us; the launch traced here: 943 us
  local copies, waits for them, and re-layouts  289 us (30%)
  matrix products  248 us (26%)
  blocking collectives  237 us (25%)
  other arithmetic  131 us (14%)
  between operations  19.6 us (2%)
  waiting for transfers between devices  17.6 us (2%)
    unnamed x2, blocking collectives  56 us
    another operation x3, local copies, waits for them, and re-layouts, per_device(): jnp.stack([shifted(odd_grad * next_low, -1), even_grad, odd_grad, shifted...  44.3 us
    dot_general x3, matrix products, per_device(): jnp.einsum('oi,bot->bit', paired_kernel_weight[block_number, 1], grad_low...  43.8 us
    slice x1, local copies, waits for them, and re-layouts, run_forward(): even_out = taps_out[:, :, 1] + shifted(taps_out[:, :, 3], -1) * in_prev  38.7 us
    dot_general x3, matrix products, run_forward(): jnp.einsum('oi,bit->bot', paired_kernel_weight[block_number, 1], hidden_l...  32.9 us
    all_gather x1, blocking collectives, gather_shards(): lax.all_gather(residual_gain, 'fsdp', axis=2, tiled=True)  32.2 us
    all_gather x1, blocking collectives, gather_shards(): lax.all_gather(paired_direction, 'fsdp', axis=3, tiled=True)  30.7 us
    all_gather x1, blocking collectives, gather_shards(): lax.all_gather(dilated_direction, 'fsdp', axis=2, tiled=True)  30.5 us
  transfers between devices with their start and end apart: 2, of which 1 were waited for; matrix products, arithmetic and copies ran while one was open for 8% of the time, Pallas kernels for 0%

commit v1 on v0

v1 whole, which is shorter than its diff:
```python
import functools
import jax, jax.numpy as jnp
from jax import lax
from jax.experimental import pallas as pl
from jax.experimental.pallas import tpu as pltpu

BF=jnp.bfloat16; F32=jnp.float32
RS=64
L=128

def dot(a,b):
    return jnp.dot(a,b,preferred_element_type=F32)
def dot_nt(a,b):
    return lax.dot_general(a,b,(((1,),(1,)),((),())),preferred_element_type=F32)

def act_pair(v):
    th=jnp.tanh(0.5*v); a=0.6+0.4*th
    return v*a, a+(0.2*v)*(1.0-th*th)

KINDS={-1:0,1:1,-2:2,2:3,-4:4,4:5,-5:6,5:7}

def main_kernel(NC, packs, cpp, *refs):
    ins=refs[:11]
    ws=ins[3:8]+(ins[8],ins[10])
    def body(masks,*sc):
        wsc=sc[:7]
        for a,b in zip(wsc,ws): a[...]=b[...]
        main_body(NC,packs,cpp,*ins[:3],*wsc[:6],ins[9],wsc[6],*refs[11:],masks,sc[7:])
    pl.run_scoped(body,pltpu.VMEM((packs*cpp,8,16,L),BF),*[pltpu.VMEM(w.shape,w.dtype) for w in ws],*[pltpu.VMEM((RS,64,L),BF)]*23)

def main_body(NC, packs, cpp, sig_h, seg, cot_h, wu, wv, wd, wdb, pf, pt, bias, perm,
                out_h, sg_h, dU, dD, dP, dB,
                sig, cot, outb, sgb, sem_in, sem_out, masks, rings):
    NCOL=packs*cpp
    (FIRST,DFIRST,PRE0,PRE1,PRE2,HID0,HID1,HID2,DH0,DH1,DH2,ACT0,ACT1,ACT2,DD0,DD1,G2,G1,G0,GD0,GD1,GD2,GU)=range(23)
    PRE=(PRE0,PRE1,PRE2);HID=(HID0,HID1,HID2);DH=(DH0,DH1,DH2);ACT=(ACT0,ACT1,ACT2);DD=(DD0,DD1);GD=(GD0,GD1,GD2);G=(G0,G1,G2)
    W=NC*L
    def copies_in(p):
        return (pltpu.make_async_copy(sig_h.at[p],sig.at[p],sem_in.at[0,p]),
                pltpu.make_async_copy(cot_h.at[p],cot.at[p],sem_in.at[1,p]))
    def copies_out(p):
        return (pltpu.make_async_copy(outb.at[p],out_h.at[p],sem_out.at[0,p]),
                pltpu.make_async_copy(sgb.at[p],sg_h.at[p],sem_out.at[1,p]))
    for p in range(packs):
        for c in copies_in(p): c.start()
    dU[...]=jnp.zeros_like(dU); dD[...]=jnp.zeros_like(dD); dP[...]=jnp.zeros_like(dP); dB[...]=jnp.zeros_like(dB)
    def zero(r,_):
        for q in rings: q[r]=jnp.zeros((64,L),BF)
        return 0
    lax.fori_loop(0,RS,zero,0)
    T=cpp*L
    for k,kind in KINDS.items():
        s=seg[...]
        pos=lax.broadcasted_iota(jnp.int32,s.shape,1)
        r=pltpu.roll(s,(-k)%T,1)
        ok=(r==s)&(pos+k>=0)&(pos+k<T)
        m=ok.astype(F32)
        for p in range(packs):
            mp=jnp.broadcast_to(m[p:p+1,:],(16,T)).astype(BF)
            for c in range(cpp):
                masks[p*cpp+c,kind]=mp[:,c*L:(c+1)*L]
    def slot(j): return j & (RS-1)
    def ld(r,j0,n=NC):
        return jnp.concatenate([rings[r][slot(j0+k)] for k in range(n)],axis=1) if n>1 else rings[r][slot(j0)]
    def st(r,j0,v):
        v=v.astype(BF)
        for k in range(NC): rings[r][slot(j0+k)]=v[:,k*L:(k+1)*L]
    def clampj(j): return jnp.clip(j,0,NCOL-1)
    def mask(kind,j0,rows):
        cols=[]
        for k in range(NC):
            m=masks[clampj(j0+k),KINDS[kind]]
            cols.append(jnp.concatenate([m]*(rows//16),axis=0))
        return jnp.concatenate(cols,axis=1)
    def shf(x,k):
        if k>0: return pltpu.roll(x[:,L:],W+L-k,1)[:,:W]
        return pltpu.roll(x[:,:W+L],-k,1)[:,L:]
    def stack(r,j0,b):
        x=ld(r,j0-1,NC+2)
        E=x[:32]; O=x[32:]
        a_=(3**b-1)//2; b_=(3**b+1)//2
        Em=x[:32,L:L+W]; Om=x[32:,L:L+W]
        Omin=shf(O,-b_)*mask(-b_,j0,32)
        Opl=shf(O,a_)*mask(a_,j0,32) if a_ else Om
        Emin=shf(E,-a_)*mask(-a_,j0,32) if a_ else Em
        Epl=shf(E,b_)*mask(b_,j0,32)
        return jnp.concatenate([Omin,Em,Opl],axis=0), jnp.concatenate([Emin,Om,Epl],axis=0)
    def per_phase(w,xE,xO): return jnp.concatenate([dot(w,xE),dot(w,xO)],axis=0)
    def rowsum(v):
        s=v[:32]+v[32:]
        r=s[:,:L]
        for k in range(1,NC): r=r+s[:,k*L:(k+1)*L]
        return r
    def bcol(i):
        x=bias[i]
        return jnp.concatenate([jnp.concatenate([x]*NC,axis=1)]*2,axis=0)
    D=NC+1
    d0=0; dl=[D*s for s in range(9)]
    def pc(j):
        jc=clampj(j)
        return jc//cpp, jc%cpp
    def po(j):
        ok=(j>=0)&(j<NCOL)
        jc=clampj(j)
        return jnp.where(ok,jc//cpp,packs), jc%cpp
    def st_V(base):
        j=base-dl[8]
        x=ld(GU,j-1,NC+2)
        gu=x[:,L:L+W]
        gt=jnp.concatenate([gu, shf(x[:32],1)*mask(1,j,32), shf(x[32:],-1)*mask(-1,j,32)],axis=0)
        fi=ld(FIRST,j); df=ld(DFIRST,j)
        y=dot(wv[...],gt)
        yield
        dU[...]+=dot_nt(gt,fi)
        yield
        sgv=(y*df.astype(F32)).astype(BF)
        for k in range(NC):
            p,c=po(j+k)
            sgb[p,:,pl.ds(pl.multiple_of(c*L,L),L)]=sgv[:,k*L:(k+1)*L]
    def st_B(base,b,si):
        j=base-dl[si]
        sE,sO=stack(GD[b],j,b)
        g=ld(G[b],j); pre=ld(PRE[b],j); dh=ld(DH[b],j); act=ld(ACT[b],j); hid=ld(HID[b],j)
        ddp=ld(DD[b-1],j) if b else None
        A=per_phase(wdb[b],sE,sO)
        S=per_phase(pt[b,1],g[:32],g[32:])
        yield
        dD[b]+=dot_nt(sE,pre[:32])+dot_nt(sO,pre[32:])
        yield
        gf=dh.astype(F32)*A+S
        gl=gf.astype(BF)
        if b==0:
            st(GU,j,gl); dB[0,2]+=rowsum(gf)
        else:
            st(G[b-1],j,gl)
            ag=per_phase(pt[b-1,0],gl[:32],gl[32:])
        yield
        dP[b]+=dot_nt(jnp.concatenate([act[:32],hid[:32]],axis=0),g[:32])+dot_nt(jnp.concatenate([act[32:],hid[32:]],axis=0),g[32:])
        if b:
            dB[b-1,1]+=rowsum(gf)
            yield
            gd=ddp.astype(F32)*ag
            dB[b-1,0]+=rowsum(gd)
            st(GD[b-1],j,gd)
    def st_D(base,b):
        j=base-dl[2+b]
        sE,sO=stack(PRE[b],j,b)
        hid=ld(HID[b],j)
        dil=per_phase(wd[b],sE,sO)
        if b==2:
            cs=[]
            for k in range(NC):
                p,c=pc(j+k)
                cs.append(cot[p,:,pl.ds(pl.multiple_of(c*2*L,2*L),2*L)])
            cz=dot(jnp.concatenate(cs,axis=0),perm[1])
        yield
        yield
        dil=dil+bcol(1+2*b)
        act,dd=act_pair(dil)
        act=act.astype(BF)
        st(ACT[b],j,act)
        h=per_phase(pf[b],jnp.concatenate([act[:32],hid[:32]],axis=0),jnp.concatenate([act[32:],hid[32:]],axis=0))
        if b<2:
            st(DD[b],j,dd)
        else:
            gE=jnp.concatenate([cz[k*32:(k+1)*32,:L] for k in range(NC)],axis=1)
            gO=jnp.concatenate([cz[k*32:(k+1)*32,L:] for k in range(NC)],axis=1)
            gf=jnp.concatenate([gE,gO],axis=0)
            vk=[jnp.where((j+k>=0)&(j+k<NCOL),1.0,0.0) for k in range(NC)]
            gf=jnp.concatenate([gf[:,k*L:(k+1)*L]*vk[k] for k in range(NC)],axis=1)
            gl=gf.astype(BF)
            st(G2,j,gl)
            dB[2,1]+=rowsum(gf)
            ag=per_phase(pt[2,0],gl[:32],gl[32:])
        yield
        yield
        h=h+bcol(2+2*b)
        if b<2:
            pre,dh=act_pair(h)
            st(PRE[b+1],j,pre); st(HID[b+1],j,h); st(DH[b+1],j,dh)
        else:
            ho=h.astype(BF)
            z=jnp.concatenate([jnp.concatenate([ho[:32,k*L:(k+1)*L],ho[32:,k*L:(k+1)*L]],axis=1) for k in range(NC)],axis=0)
            z=dot(z,perm[0])
            gd=dd*ag
            dB[2,0]+=rowsum(gd)
            st(GD2,j,gd)
            yield
            z=z.astype(BF)
            for k in range(NC):
                p,c=po(j+k)
                outb[p,:,pl.ds(pl.multiple_of(c*2*L,2*L),2*L)]=z[k*32:(k+1)*32]
    def st_U(base):
        j=base-dl[1]
        x=ld(FIRST,j-1,NC+2)
        f0=x[:,L:L+W]
        fm=shf(x,-1)*mask(-1,j,64); fp=shf(x,1)*mask(1,j,64)
        h=jnp.concatenate([dot(wu[0],jnp.concatenate([f0,fm],axis=0)),dot(wu[1],jnp.concatenate([f0,fp],axis=0))],axis=0)
        yield
        yield
        h=h+bcol(0)
        pre,dh=act_pair(h)
        st(PRE0,j,pre); st(HID0,j,h); st(DH0,j,dh)
    def st_F(base):
        j=base
        xs=[]
        for k in range(NC):
            p,c=pc(j+k)
            xs.append(sig[p,:,pl.ds(pl.multiple_of(c*L,L),L)])
        x=jnp.concatenate(xs,axis=1)
        yield
        fv,dv=act_pair(x.astype(F32))
        st(FIRST,j,fv); st(DFIRST,j,dv)
    def step(i,_):
        base=i*NC
        gens=[st_V(base),st_D(base,2),st_B(base,0,7),st_B(base,1,6),st_D(base,1),st_B(base,2,5),st_D(base,0),st_U(base),st_F(base)]
        while gens:
            nxt=[]
            for g in gens:
                try: next(g); nxt.append(g)
                except StopIteration: pass
            gens=nxt
        return 0
    ipp=cpp//NC
    def outer(g,_):
        for c in copies_in(g): c.wait()
        lax.fori_loop(g*ipp,(g+1)*ipp,step,0)
        @pl.when(g>=2)
        def _():
            for c in copies_out(g-2): c.start()
        return 0
    lax.fori_loop(0,packs,outer,0)
    tot=packs*ipp-(-dl[8]//NC)
    lax.fori_loop(packs*ipp,tot,step,0)
    for p in (packs-2,packs-1):
        for c in copies_out(p): c.start()
    for p in range(packs):
        for c in copies_out(p): c.wait()

def make_perm():
    r=jnp.arange(2*L)[:,None]; c=jnp.arange(2*L)[None,:]
    tgt=jnp.where(r<L,2*r,2*(r-L)+1)
    P=(tgt==c).astype(BF)
    return jnp.stack([P,P.T])

def prep(uw,dw,pw,ub,rb):
    taps=uw.reshape(64,32,4)
    t=[taps[:,:,k] for k in range(4)]
    wu=jnp.stack([jnp.concatenate([t[1].T,t[3].T],1),jnp.concatenate([t[2].T,t[0].T],1)])
    wv=jnp.concatenate([t[1],t[2],t[3],t[0]],1)
    d3=dw.reshape(3,32,3,32)
    wdb=jnp.concatenate([d3[:,:,2].transpose(0,2,1),d3[:,:,1].transpose(0,2,1),d3[:,:,0].transpose(0,2,1)],2)
    pf=jnp.concatenate([pw[:,0],pw[:,1]],2)
    pt=pw.transpose(0,1,3,2)
    ub=ub.astype(F32); rb=rb.astype(F32)
    bl=[ub]
    for b in range(3): bl+= [rb[b,0], rb[b,1]+rb[b,2]]
    bias=jnp.broadcast_to(jnp.stack(bl)[:,:,None],(7,32,L))
    return wu,wv,dw,wdb,pf,pt,bias

def main_call(NC,signal,segments,cot,wts):
    packs,cin,T=signal.shape
    cpp=T//L
    wu,wv,wd,wdb,pf,pt,bias=wts
    perm=make_perm()
    V=pl.BlockSpec(memory_space=pltpu.VMEM); A=pl.BlockSpec(memory_space=pl.ANY)
    return pl.pallas_call(
        functools.partial(main_kernel,NC,packs,cpp),
        name="section",
        out_shape=(jax.ShapeDtypeStruct(cot.shape,BF),jax.ShapeDtypeStruct(signal.shape,BF),
            jax.ShapeDtypeStruct((128,64),F32),jax.ShapeDtypeStruct((3,96,32),F32),jax.ShapeDtypeStruct((3,64,32),F32),jax.ShapeDtypeStruct((3,3,32,L),F32)),
        in_specs=[A,V,A]+[V]*8, out_specs=(A,A,V,V,V,V),
        scratch_shapes=[pltpu.VMEM(signal.shape,BF),pltpu.VMEM(cot.shape,BF),
            pltpu.VMEM((packs+1,32,2*T),BF),pltpu.VMEM((packs+1,64,T),BF),
            pltpu.SemaphoreType.DMA((2,packs)),pltpu.SemaphoreType.DMA((2,packs))],
        compiler_params=pltpu.CompilerParams(vmem_limit_bytes=63<<20),
    )(signal,segments,cot,wu,wv,wd,wdb,pf,pt,bias,perm)

from jax.sharding import PartitionSpec as P


def pack_local(ud, ug, ub, dd, pd, rg, rb):
    return jnp.concatenate([v.reshape(-1) for v in (ud, dd, pd, ug, ub, rg, rb)])


def norm_backward(direction, scale, norm, weight_grad):
    inner = jnp.sum(weight_grad * direction, axis=-1, keepdims=True)
    scale_grad = (inner / norm)[..., 0]
    return scale / norm * (weight_grad - inner / (norm * norm) * direction), scale_grad


def per_device(nd, nf, signal, segments, cotangent, ud, ug, ub, dd, pd, rg, rb):
    shards = (ud, dd, pd, ug, ub, rg, rb)
    flat = pack_local(ud, ug, ub, dd, pd, rg, rb)
    full = lax.all_gather(flat, ("dp", "fsdp"), axis=0, tiled=False).reshape(nd, nf, -1)
    sizes = [v.size for v in shards]
    parts, at = [], 0
    for v, n in zip(shards, sizes):
        parts.append(full[:, :, at:at + n].reshape((nd, nf) + v.shape))
        at += n
    ud_f = parts[0].transpose(0, 2, 1, 3).reshape(64, 128).astype(F32)
    dd_f = parts[1].transpose(2, 0, 3, 1, 4).reshape(3, 32, 96).astype(F32)
    pd_f = parts[2].transpose(2, 3, 0, 4, 1, 5).reshape(3, 2, 32, 32).astype(F32)
    ug_f = parts[3][0].reshape(64).astype(F32)
    ub_f = parts[4][0].reshape(32)
    rg_f = parts[5][0].transpose(1, 2, 0, 3).reshape(3, 3, 32).astype(F32)
    rb_f = parts[6][0].transpose(1, 2, 0, 3).reshape(3, 3, 32)
    un = jnp.sqrt(jnp.sum(ud_f * ud_f, axis=1, keepdims=True))
    dn = jnp.sqrt(jnp.sum(dd_f * dd_f, axis=2, keepdims=True))
    pn = jnp.sqrt(jnp.sum(pd_f * pd_f, axis=3, keepdims=True))
    us, ds, ps = ug_f[:, None], rg_f[:, 0, :, None], rg_f[:, 1:, :, None]
    wts = prep((us * ud_f / un).astype(BF), (ds * dd_f / dn).astype(BF), (ps * pd_f / pn).astype(BF), ub_f, rb_f)
    out, sg, gu, gd, gp, gb = main_call(NC, signal, segments, cotangent, wts)
    gu = gu.reshape(4, 32, 64)[jnp.array([3, 0, 1, 2])].transpose(2, 1, 0).reshape(64, 128)
    gd = gd.reshape(3, 3, 32, 32)[:, ::-1].transpose(0, 2, 1, 3).reshape(3, 32, 96)
    gp = gp.reshape(3, 2, 32, 32).transpose(0, 1, 3, 2)
    gb = gb.sum(-1)
    gud, gug = norm_backward(ud_f, us, un, gu)
    gdd, gdg = norm_backward(dd_f, ds, dn, gd)
    gpd, gpg = norm_backward(pd_f, ps, pn, gp)
    grg = jnp.concatenate([gdg[:, None], gpg], axis=1)
    grb = jnp.stack([gb[:, 0], gb[:, 1], gb[:, 1]], axis=1)
    a, b = ud.shape
    m0 = gud.reshape(nd, a, nf, b).transpose(0, 2, 1, 3).reshape(nd, nf, -1)
    a, b = dd.shape[1:]
    m1 = gdd.reshape(3, nd, a, nf, b).transpose(1, 3, 0, 2, 4).reshape(nd, nf, -1)
    a, b = pd.shape[2:]
    m2 = gpd.reshape(3, 2, nd, a, nf, b).transpose(2, 4, 0, 1, 3, 5).reshape(nd, nf, -1)
    sm = [gug.reshape(nf, -1), gb[0, 2].reshape(nf, -1), grg.reshape(9, nf, -1).transpose(1, 0, 2).reshape(nf, -1),
          grb.reshape(9, nf, -1).transpose(1, 0, 2).reshape(nf, -1)]
    sm = jnp.broadcast_to(jnp.concatenate(sm, axis=1)[None], (nd, nf, sum(v.shape[1] for v in sm)))
    msg = jnp.concatenate([m0, m1, m2, sm], axis=2).reshape(nd * nf, -1)
    tot = lax.psum_scatter(msg, ("dp", "fsdp"), scatter_dimension=0, tiled=True)[0]
    res, at = [], 0
    for v, n in zip(shards, sizes):
        res.append(tot[at:at + n].reshape(v.shape))
        at += n
    return out, sg, res[0], res[3], res[4], res[1], res[2], res[5], res[6]


NC = 4


def solution(mesh):
    nd, nf = mesh.shape["dp"], mesh.shape["fsdp"]
    return jax.shard_map(
        functools.partial(per_device, nd, nf),
        mesh=mesh,
        in_specs=(
            P(("dp", "fsdp"), None, None),
            P(("dp", "fsdp"), None),
            P(("dp", "fsdp"), None, None),
            P("dp", "fsdp"),
            P("fsdp"),
            P("fsdp"),
            P(None, "dp", "fsdp"),
            P(None, None, "dp", "fsdp"),
            P(None, None, "fsdp"),
            P(None, None, "fsdp"),
        ),
        out_specs=(
            P(("dp", "fsdp"), None, None),
            P(("dp", "fsdp"), None, None),
            P("dp", "fsdp"),
            P("fsdp"),
            P("fsdp"),
            P(None, "dp", "fsdp"),
            P(None, None, "dp", "fsdp"),
            P(None, None, "fsdp"),
            P(None, None, "fsdp"),
        ),
        check_vma=False,
    )
```

time: 955 us -> 309 us (0.32); the launches traced: 943 us -> 307 us
  local copies, waits for them, and re-layouts: 289 us -> 27.2 us
  matrix products: 248 us -> 0 us
  blocking collectives: 237 us -> 42.5 us
  other arithmetic: 131 us -> 10.4 us
  waiting for transfers between devices: 17.6 us -> 121 us
  Pallas kernels: 0 us -> 91.7 us
    dot_general x30 -> x0, matrix products: 248 us -> none  [the longest x3 43.8 us: per_device(): jnp.einsum('oi,bot->bit', paired_kernel_weight[block_number, 1], grad_low...]
    all_gather x8 -> x0, blocking collectives: 170 us -> none  [the longest x1 32.2 us: gather_shards(): lax.all_gather(residual_gain, 'fsdp', axis=2, tiled=True)]
    unnamed x3 -> x2, waiting for transfers between devices: 0.03 us -> 121 us
    pallas_call x0 -> x1, Pallas kernels: none -> 91.7 us  [main_call(): pl.pallas_call(functools.partial(main_kernel, NC, packs, cpp), name='sect...]
    mul x14 -> x1, other arithmetic: 82.8 us -> 0.02 us  [norm_backward(): scale / norm * (weight_grad - inner / (norm * norm) * direction)]
    slice x22 -> x10, local copies, waits for them, and re-layouts: 78.9 us -> 5.78 us  [the longest x6 5.73 us: per_device(): res.append(tot[at:at + n].reshape(v.shape))]
    another operation x4 -> x3, local copies, waits for them, and re-layouts: 67.5 us -> 0.2 us  [the longest x1 0.09 us: per_device(): us, ds, ps = (ug_f[:, None], rg_f[:, 0, :, None], rg_f[:, 1:, :, None])]
    reshape x3 -> x22, local copies, waits for them, and re-layouts: 53.2 us -> 8.54 us  [the longest x5 3.23 us: pack_local(): v.reshape(-1)]
  transfers between devices with their start and end apart: 2 -> 1, of which waited for: 1 -> 1; matrix products, arithmetic and copies ran while one was open for 8% -> 0% of each run, Pallas kernels for 0% -> 0%
where the time goes in v1:
time: 309 us; the launch traced here: 307 us
  waiting for transfers between devices  121 us (39%)
  Pallas kernels  91.7 us (30%)
  blocking collectives  42.5 us (14%)
  local copies, waits for them, and re-layouts  27.2 us (9%)
  between operations  14.5 us (5%)
  other arithmetic  10.4 us (3%)
    unnamed x2, waiting for transfers between devices  121 us
    pallas_call x1, Pallas kernels, main_call(): pl.pallas_call(functools.partial(main_kernel, NC, packs, cpp), name='sect...  91.7 us
    unnamed x1, blocking collectives  42.5 us
  transfers between devices with their start and end apart: 1, of which 1 were waited for; matrix products, arithmetic and copies ran while one was open for 0% of the time, Pallas kernels for 0%

profile of v1, /device:TPU:0, one launch (start us, length us, event | category | flops | bytes accessed | tf_op | source)
XLA Modules:
  0.0 307.1 jit_solution(17843288502718826071)
XLA Ops:
  7.2 0.8 copy.136
  8.2 0.8 reshape.461
  9.0 0.8 reshape.460
  9.7 0.8 reshape.463
  10.5 0.8 reshape.464
  11.3 1.4 concatenate.36
  12.7 0.2 dynamic-update-slice
  12.9 42.5 %all-reduce = bf16[26240]{0:T(1024)(128)(2,1)S(1)} all-reduce(bf16[26240]{0:T(1024)(128)(2,1)S(1)} %dynamic-update-slice), channel_id=2, replica_groups=mesh['dp'=4,'fsdp'=8] {'dp','fsdp'}, use_global_device_ids=true, to_apply=%add | all-reduce | flops 26240 | bytes 104960
  55.5 0.2 reshape.465
  55.8 0.1 copy.137
  56.5 0.2 reshape.494
  56.7 0.1 multiply_reduce_fusion
  56.9 0.2 reshape.485
  57.1 0.2 reshape.484
  57.4 0.1 copy.144
  58.0 0.6 slice_multiply_fusion
  58.5 0.2 copy.149
  58.7 0.3 copy.150
  59.0 0.2 reshape.486
  59.3 0.6 fusion.12.refs_8_
  60.1 0.7 reshape.489
  60.7 0.2 reshape.482
  60.9 0.6 copy-done
  62.7 0.1 copy.154
  63.0 0.7 copy.155.refs_7_
  63.7 0.7 divide_convert_fusion.3.refs_5_
  64.5 0.6 pad_clamp_fusion
  65.2 0.6 pad_maximum_fusion.3.refs_3_
  65.8 0.7 add_convert_fusion.refs_10_
  66.5 0.7 pad_maximum_fusion.2.refs_6_
  67.2 0.7 pad_maximum_fusion.4.refs_4_
  67.9 0.8 broadcast_in_dim.6.refs_9_
  68.7 91.7 %section.1 = (bf16[8,32,8192]{2,1,0:T(8,128)(2,1)}, bf16[8,64,4096]{2,1,0:T(8,128)(2,1)}, f32[128,64]{1,0:T(8,128)}, f32[3,96,32]{2,1,0:T(8,128)}, f32[3,64,32]{2,1,0:T(8,128)}, /*index=5*/f32[3,3,32,128]{3,2,1,0:T(8,128)}) custom-call(bf16[8,64,4096]{2,1,0:T(8,128)(2,1)} %refs_0_.1, s32[8,4096]{1,0:T(8,128)} %refs_1_.1, bf16[8,32,8192]{2,1,0:T(8,128)(2,1)} %refs_2_.1, ...), custom_call_target="tpu_custom_call" | custom-call | tf_op jit(solution)/shard_map/section/pallas_call | solution.py:267
  160.4 1.6 gather_fusion
  161.9 0.9 fusion.4
  163.0 1.0 reduce_sum.89
  164.1 0.2 reshape.467
  164.3 0.7 rsqrt_multiply_fusion
  165.1 0.1 copy.159
  165.2 0.1 concatenate.42
  165.4 1.0 copy.163
  166.4 0.2 rev.3
  166.6 0.3 multiply_reduce_fusion.2
  167.1 0.2 reshape.469
  167.3 0.2 fusion.1
  167.5 0.2 concatenate.43
  167.7 0.2 reshape.471
  168.0 0.3 copy.167
  168.3 0.2 concatenate.44
  168.9 0.1 copy.170
  169.2 0.1 copy.171
  169.6 0.7 pad_maximum_fusion
  170.3 120.6 %all-reduce.4.cloned.1.call-done = f32[32,820]{1,0:T(8,128)} async-done(((f32[32,820]{1,0:T(8,128)}), f32[32,820]{1,0:T(8,128)}) %all-reduce.4.cloned.1.call-update) | async-done | bytes 104976
  291.0 0.8 dynamic-slice_reduce_fusion.1
  291.9 0.7 copy.175
  292.6 0.8 dynamic-slice_reduce_fusion
  293.4 0.7 reshape.477
  294.1 0.7 dynamic-slice_reduce_fusion.2
  294.8 0.7 reshape.476
  295.5 0.9 dynamic-slice_reduce_fusion.3
  296.4 0.7 reshape.479
  297.1 0.7 reshape.480
  297.7 1.3 dynamic-slice_bitcast_fusion
  299.0 1.3 dynamic-slice_bitcast_fusion.1
  (94 shorter events, 4.5 us)
Async XLA Ops:
  7.2 283.8 %all-reduce.4.cloned.1.call-start = ((), (), s32[]{:S(2)}) async-start(), calls=%async_computation | async-start | bytes 229376
  55.8 8.7 %copy-start.4 = (s32[4]{0:T(128)S(1)}, s32[4]{0:T(128)}, u32[]{:S(2)}) copy-start(s32[4]{0:T(128)} %constant.29) | copy-start | bytes 52
  56.1 11.1 %copy-start.2 = (f32[4,16]{1,0:T(4,128)}, f32[4,16]{1,0:T(4,128)S(1)}, u32[]{:S(2)}) copy-start(f32[4,16]{1,0:T(4,128)S(1)} %multiply_reduce_fusion.1) | copy-start | bytes 772
  60.9 0.6 copy-start
  160.4 7.3 %copy-start.1 = (f32[3,64,32]{2,1,0:T(8,128)S(1)}, f32[3,64,32]{2,1,0:T(8,128)}, u32[]{:S(2)}) copy-start(f32[3,64,32]{2,1,0:T(8,128)} %get-tuple-element.19) | copy-start | bytes 73732
  160.4 7.3 %copy-start.3 = (f32[3,2,32]{2,1,0:T(2,128)S(1)}, f32[3,2,32]{2,1,0:T(2,128)}, u32[]{:S(2)}) copy-start(f32[3,2,32]{2,1,0:T(2,128)} %get-tuple-element.79) | copy-start | bytes 2308
Sparse Core Ops, SparseCore 0:
  170.5 120.4 all-reduce.3

commit v2 on v1

--- a/solution.py
+++ b/solution.py
@@ -19,18 +19,166 @@
 
 KINDS={-1:0,1:1,-2:2,2:3,-4:4,4:5,-5:6,5:7}
 
-def main_kernel(NC, packs, cpp, *refs):
-    ins=refs[:11]
-    ws=ins[3:8]+(ins[8],ins[10])
-    def body(masks,*sc):
-        wsc=sc[:7]
-        for a,b in zip(wsc,ws): a[...]=b[...]
-        main_body(NC,packs,cpp,*ins[:3],*wsc[:6],ins[9],wsc[6],*refs[11:],masks,sc[7:])
-    pl.run_scoped(body,pltpu.VMEM((packs*cpp,8,16,L),BF),*[pltpu.VMEM(w.shape,w.dtype) for w in ws],*[pltpu.VMEM((RS,64,L),BF)]*23)
-
-def main_body(NC, packs, cpp, sig_h, seg, cot_h, wu, wv, wd, wdb, pf, pt, bias, perm,
-                out_h, sg_h, dU, dD, dP, dB,
-                sig, cot, outb, sgb, sem_in, sem_out, masks, rings):
+class Lay:
+    def __init__(self, nd, nf):
+        self.nd, self.nf, self.n = nd, nf, nd * nf
+        self.wu, self.wd, self.wp, self.wr, self.wg = 128 // nf, 96 // nf, 32 // nf, 32 // nf, 64 // nf
+        self.pu = 64 // nd // 8
+        at = 0
+        self.u = []
+        for _ in range(self.pu):
+            self.u.append(at)
+            at += self.wu
+        self.d = []
+        for _ in range(3):
+            self.d.append(at)
+            at += self.wd
+        self.p = []
+        for _ in range(6):
+            self.p.append(at)
+            at += self.wp
+        self.r = []
+        for _ in range(3):
+            self.r.append(at)
+            at += self.wr
+        self.g = at
+        assert at + self.wg <= 128
+
+
+def lane8(): return lax.broadcasted_iota(jnp.int32,(8,L),1)
+
+
+def move(x, frm, to):
+    k=(to-frm)%L
+    return x if k==0 else pltpu.roll(x,k,1)
+
+
+def put(acc, x, frm, to, w):
+    lane=lane8()
+    return jnp.where((lane>=to)&(lane<to+w),move(x,frm,to),acc)
+
+
+def tap_perm():
+    r=lax.broadcasted_iota(jnp.int32,(L,L),0); c=lax.broadcasted_iota(jnp.int32,(L,L),1)
+    pos=((r&3)+3)&3
+    return (c==pos*32+(r>>2)).astype(F32).astype(BF)
+
+
+def square(x):
+    return jnp.concatenate([x,jnp.zeros((L-x.shape[0],L),F32)],axis=0) if x.shape[0]<L else x
+
+
+def prologue(lay, recv, wu, wv, wd, wdb, pf, pt, bias, dirs, cols):
+    nd,nf=lay.nd,lay.nf
+    z=jnp.zeros((8,L),F32)
+    def gather(i, o, w, off=0, acc=None):
+        acc=z if acc is None else acc
+        for f in range(nf):
+            acc=put(acc,recv[i*nf+f].astype(F32),o,off+f*w,w)
+        return acc
+    ud=jnp.concatenate([gather(i,o,lay.wu) for i in range(nd) for o in lay.u],axis=0)
+    dd=[jnp.concatenate([gather(i,lay.d[b],lay.wd) for i in range(nd)],axis=0) for b in range(3)]
+    pd=[jnp.concatenate([gather(i,lay.p[2*b+1],lay.wp,32,gather(i,lay.p[2*b],lay.wp)) for i in range(nd)],axis=0) for b in range(3)]
+    sm=[gather(0,lay.r[b],lay.wr) for b in range(3)]+[gather(0,lay.g,lay.wg),gather(0,lay.g,lay.wr)]
+    st=square(jnp.concatenate(sm,axis=0)).T
+    def col(q,rows): return jnp.broadcast_to(st[:rows,q:q+1],(rows,L))
+    def norm(x): return jnp.broadcast_to(jnp.sqrt(jnp.sum(x*x,axis=1,keepdims=True)),x.shape)
+    n=norm(ud); g=col(24,64)
+    dirs[0:64]=ud; cols[0,0:64]=g/n; cols[1,0:64]=1.0/n
+    w=dot((g*ud/n).astype(BF),tap_perm())
+    wv[...]=w.astype(BF)
+    m=jnp.concatenate([w,pltpu.roll(w,64,1)],axis=0).T
+    wu[0]=m[:32].astype(BF); wu[1]=m[32:64].astype(BF)
+    bias[0]=col(33,32)
+    lane=lax.broadcasted_iota(jnp.int32,(32,L),1)
+    for b in range(3):
+        r=64+32*b
+        x=dd[b]; n=norm(x); g=col(8*b,32)
+        dirs[r:r+32]=x; cols[0,r:r+32]=g/n; cols[1,r:r+32]=1.0/n
+        w=(g*x/n).astype(BF)
+        wd[b]=w[:,:96]
+        w=w.astype(F32)
+        m=square(jnp.concatenate([pltpu.roll(w,64,1),pltpu.roll(w,96,1),w],axis=0)).T
+        wdb[b]=m[:32,:96].astype(BF)
+        r=160+32*b
+        x=pd[b]
+        n=jnp.where(lane<32,norm(jnp.where(lane<32,x,0.0)),norm(jnp.where(lane<32,0.0,x)))
+        g=jnp.where(lane<32,col(8*b+1,32),col(8*b+2,32))
+        dirs[r:r+32]=x; cols[0,r:r+32]=g/n; cols[1,r:r+32]=1.0/n
+        w=(g*x/n).astype(BF)
+        pf[b]=w[:,:64]
+        m=square(w.astype(F32)).T
+        pt[b]=m[:64,:32].astype(BF)
+        bias[1+2*b]=col(8*b+3,32)
+        bias[2+2*b]=col(8*b+4,32)+col(8*b+5,32)
+
+
+def epilogue(lay, dU, dD, dP, dB, dirs, cols, tmp, msgs):
+    nd,nf=lay.nd,lay.nf
+    def rs(x): return jnp.sum(x,axis=1,keepdims=True)
+    lane=lax.broadcasted_iota(jnp.int32,(64,L),1); lane32=lane[:32]
+    C=jnp.zeros((64,L),F32)
+    def place(C,q,c):
+        c=jnp.broadcast_to(c,(c.shape[0],L))
+        if c.shape[0]==32: c=jnp.concatenate([c,jnp.zeros((32,L),F32)],axis=0)
+        return jnp.where(lane==q,c,C)
+    perm=tap_perm()
+    v=dot(dirs[0:64].astype(BF),perm); w=dU[...]; s=cols[0,0:64]; i=cols[1,0:64]
+    inner=rs(w*v)
+    C=place(C,24,inner*i)
+    g=s*(w-(inner*i*i)*v)
+    gu=dot_nt(g.astype(BF),perm)
+    gd=[];gp=[]
+    tmp[...]=jnp.zeros_like(tmp)
+    for b in range(3):
+        r=64+32*b
+        for t in range(3): tmp[b,:,t*32:t*32+32]=dD[b,(2-t)*32:(3-t)*32]
+        v=dirs[r:r+32]; w=tmp[b]; s=cols[0,r:r+32]; i=cols[1,r:r+32]
+        inner=rs(w*v)
+        C=place(C,8*b,inner*i)
+        gd.append(s*(w-(inner*i*i)*v))
+        r=160+32*b
+        tmp[3+b,:,:64]=dP[b]
+        v=dirs[r:r+32]; w=tmp[3+b]; s=cols[0,r:r+32]; i=cols[1,r:r+32]
+        p=w*v
+        inner=jnp.where(lane32<32,rs(jnp.where(lane32<32,p,0.0)),rs(jnp.where(lane32<32,0.0,p)))
+        C=place(C,8*b+1,inner[:,:1]*i[:,:1])
+        C=place(C,8*b+2,inner[:,32:33]*i[:,32:33])
+        gp.append(s*(w-(inner*i*i)*v))
+        C=place(C,8*b+3,rs(dB[b,0]))
+        o=rs(dB[b,1])
+        C=place(C,8*b+4,o); C=place(C,8*b+5,o)
+    C=place(C,33,rs(dB[0,2]))
+    S=square(C).T
+    for f in range(nf):
+        sm=jnp.zeros((8,L),F32)
+        for b in range(3): sm=put(sm,S[8*b:8*b+8],f*lay.wr,lay.r[b],lay.wr)
+        sm=put(sm,S[24:32],f*lay.wg,lay.g,lay.wg)
+        row=lax.broadcasted_iota(jnp.int32,(8,L),0)
+        sm=jnp.where(row==1,put(sm,S[32:40],f*lay.wr,lay.g,lay.wr),sm)
+        for d in range(nd):
+            x=sm
+            for p in range(lay.pu): x=put(x,gu[(d*lay.pu+p)*8:(d*lay.pu+p)*8+8],f*lay.wu,lay.u[p],lay.wu)
+            for b in range(3):
+                x=put(x,gd[b][8*d:8*d+8],f*lay.wd,lay.d[b],lay.wd)
+                for j in range(2): x=put(x,gp[b][8*d:8*d+8],32*j+f*lay.wp,lay.p[2*b+j],lay.wp)
+            msgs[d*nf+f]=x.astype(BF)
+
+
+def main_kernel(NC, packs, cpp, lay, sig_h, seg, cot_h, recv, perm_in, out_h, sg_h, msgs,
+                sig, cot, outb, sgb, dU, dD, dP, dB, dirs, cols, tmp, bias, sem_in, sem_out):
+    def body(masks, wu, wv, wd, wdb, pf, pt, perm, *rings):
+        perm[...]=perm_in[...]
+        main_body(NC,packs,cpp,lay,recv,sig_h,seg,cot_h,wu,wv,wd,wdb,pf,pt,bias,perm,out_h,sg_h,msgs,dU,dD,dP,dB,
+                  sig,cot,outb,sgb,dirs,cols,tmp,sem_in,sem_out,masks,rings)
+    pl.run_scoped(body,pltpu.VMEM((packs*cpp,8,16,L),BF),
+                  pltpu.VMEM((2,32,L),BF),pltpu.VMEM((64,L),BF),pltpu.VMEM((3,32,96),BF),pltpu.VMEM((3,32,96),BF),
+                  pltpu.VMEM((3,32,64),BF),pltpu.VMEM((3,64,32),BF),pltpu.VMEM((2,2*L,2*L),BF),
+                  *[pltpu.VMEM((RS,64,L),BF)]*23)
+
+
+def main_body(NC, packs, cpp, lay, recv, sig_h, seg, cot_h, wu, wv, wd, wdb, pf, pt, bias, perm,
+              out_h, sg_h, msgs, dU, dD, dP, dB, sig, cot, outb, sgb, dirs, cols, tmp, sem_in, sem_out, masks, rings):
     NCOL=packs*cpp
     (FIRST,DFIRST,PRE0,PRE1,PRE2,HID0,HID1,HID2,DH0,DH1,DH2,ACT0,ACT1,ACT2,DD0,DD1,G2,G1,G0,GD0,GD1,GD2,GU)=range(23)
     PRE=(PRE0,PRE1,PRE2);HID=(HID0,HID1,HID2);DH=(DH0,DH1,DH2);ACT=(ACT0,ACT1,ACT2);DD=(DD0,DD1);GD=(GD0,GD1,GD2);G=(G0,G1,G2)
@@ -43,6 +191,7 @@
                 pltpu.make_async_copy(sgb.at[p],sg_h.at[p],sem_out.at[1,p]))
     for p in range(packs):
         for c in copies_in(p): c.start()
+    prologue(lay,recv,wu,wv,wd,wdb,pf,pt,bias,dirs,cols)
     dU[...]=jnp.zeros_like(dU); dD[...]=jnp.zeros_like(dD); dP[...]=jnp.zeros_like(dP); dB[...]=jnp.zeros_like(dB)
     def zero(r,_):
         for q in rings: q[r]=jnp.zeros((64,L),BF)
@@ -111,7 +260,7 @@
         fi=ld(FIRST,j); df=ld(DFIRST,j)
         y=dot(wv[...],gt)
         yield
-        dU[...]+=dot_nt(gt,fi)
+        dU[...]+=dot_nt(fi,gt)
         yield
         sgv=(y*df.astype(F32)).astype(BF)
         for k in range(NC):
@@ -123,7 +272,7 @@
         g=ld(G[b],j); pre=ld(PRE[b],j); dh=ld(DH[b],j); act=ld(ACT[b],j); hid=ld(HID[b],j)
         ddp=ld(DD[b-1],j) if b else None
         A=per_phase(wdb[b],sE,sO)
-        S=per_phase(pt[b,1],g[:32],g[32:])
+        S=per_phase(pt[b,32:],g[:32],g[32:])
         yield
         dD[b]+=dot_nt(sE,pre[:32])+dot_nt(sO,pre[32:])
         yield
@@ -133,9 +282,9 @@
             st(GU,j,gl); dB[0,2]+=rowsum(gf)
         else:
             st(G[b-1],j,gl)
-            ag=per_phase(pt[b-1,0],gl[:32],gl[32:])
-        yield
-        dP[b]+=dot_nt(jnp.concatenate([act[:32],hid[:32]],axis=0),g[:32])+dot_nt(jnp.concatenate([act[32:],hid[32:]],axis=0),g[32:])
+            ag=per_phase(pt[b-1,:32],gl[:32],gl[32:])
+        yield
+        dP[b]+=dot_nt(g[:32],jnp.concatenate([act[:32],hid[:32]],axis=0))+dot_nt(g[32:],jnp.concatenate([act[32:],hid[32:]],axis=0))
         if b:
             dB[b-1,1]+=rowsum(gf)
             yield
@@ -171,7 +320,7 @@
             gl=gf.astype(BF)
             st(G2,j,gl)
             dB[2,1]+=rowsum(gf)
-            ag=per_phase(pt[2,0],gl[:32],gl[32:])
+            ag=per_phase(pt[2,:32],gl[:32],gl[32:])
         yield
         yield
         h=h+bcol(2+2*b)
@@ -234,6 +383,7 @@
     lax.fori_loop(packs*ipp,tot,step,0)
     for p in (packs-2,packs-1):
         for c in copies_out(p): c.start()
+    epilogue(lay,dU,dD,dP,dB,dirs,cols,tmp,msgs)
     for p in range(packs):
         for c in copies_out(p): c.wait()
 
@@ -243,108 +393,149 @@
     P=(tgt==c).astype(BF)
     return jnp.stack([P,P.T])
 
-def prep(uw,dw,pw,ub,rb):
-    taps=uw.reshape(64,32,4)
-    t=[taps[:,:,k] for k in range(4)]
-    wu=jnp.stack([jnp.concatenate([t[1].T,t[3].T],1),jnp.concatenate([t[2].T,t[0].T],1)])
-    wv=jnp.concatenate([t[1],t[2],t[3],t[0]],1)
-    d3=dw.reshape(3,32,3,32)
-    wdb=jnp.concatenate([d3[:,:,2].transpose(0,2,1),d3[:,:,1].transpose(0,2,1),d3[:,:,0].transpose(0,2,1)],2)
-    pf=jnp.concatenate([pw[:,0],pw[:,1]],2)
-    pt=pw.transpose(0,1,3,2)
-    ub=ub.astype(F32); rb=rb.astype(F32)
-    bl=[ub]
-    for b in range(3): bl+= [rb[b,0], rb[b,1]+rb[b,2]]
-    bias=jnp.broadcast_to(jnp.stack(bl)[:,:,None],(7,32,L))
-    return wu,wv,dw,wdb,pf,pt,bias
-
-def main_call(NC,signal,segments,cot,wts):
+
+def main_call(NC, lay, signal, segments, cot, recv):
     packs,cin,T=signal.shape
     cpp=T//L
-    wu,wv,wd,wdb,pf,pt,bias=wts
-    perm=make_perm()
     V=pl.BlockSpec(memory_space=pltpu.VMEM); A=pl.BlockSpec(memory_space=pl.ANY)
     return pl.pallas_call(
-        functools.partial(main_kernel,NC,packs,cpp),
+        functools.partial(main_kernel,NC,packs,cpp,lay),
         name="section",
-        out_shape=(jax.ShapeDtypeStruct(cot.shape,BF),jax.ShapeDtypeStruct(signal.shape,BF),
-            jax.ShapeDtypeStruct((128,64),F32),jax.ShapeDtypeStruct((3,96,32),F32),jax.ShapeDtypeStruct((3,64,32),F32),jax.ShapeDtypeStruct((3,3,32,L),F32)),
-        in_specs=[A,V,A]+[V]*8, out_specs=(A,A,V,V,V,V),
+        out_shape=(jax.ShapeDtypeStruct(cot.shape,BF),jax.ShapeDtypeStruct(signal.shape,BF),jax.ShapeDtypeStruct((lay.n,8,L),BF)),
+        in_specs=[A,V,A,V,V], out_specs=(A,A,V),
         scratch_shapes=[pltpu.VMEM(signal.shape,BF),pltpu.VMEM(cot.shape,BF),
             pltpu.VMEM((packs+1,32,2*T),BF),pltpu.VMEM((packs+1,64,T),BF),
+            pltpu.VMEM((64,L),F32),pltpu.VMEM((3,96,32),F32),pltpu.VMEM((3,32,64),F32),pltpu.VMEM((3,3,32,L),F32),
+            pltpu.VMEM((256,L),F32),pltpu.VMEM((2,256,L),F32),pltpu.VMEM((6,32,L),F32),pltpu.VMEM((7,32,L),F32),
             pltpu.SemaphoreType.DMA((2,packs)),pltpu.SemaphoreType.DMA((2,packs))],
         compiler_params=pltpu.CompilerParams(vmem_limit_bytes=63<<20),
-    )(signal,segments,cot,wu,wv,wd,wdb,pf,pt,bias,perm)
+    )(signal,segments,cot,recv,make_perm())
 
 from jax.sharding import PartitionSpec as P
 
-
-def pack_local(ud, ug, ub, dd, pd, rg, rb):
-    return jnp.concatenate([v.reshape(-1) for v in (ud, dd, pd, ug, ub, rg, rb)])
-
-
-def norm_backward(direction, scale, norm, weight_grad):
-    inner = jnp.sum(weight_grad * direction, axis=-1, keepdims=True)
-    scale_grad = (inner / norm)[..., 0]
-    return scale / norm * (weight_grad - inner / (norm * norm) * direction), scale_grad
-
-
-def per_device(nd, nf, signal, segments, cotangent, ud, ug, ub, dd, pd, rg, rb):
-    shards = (ud, dd, pd, ug, ub, rg, rb)
-    flat = pack_local(ud, ug, ub, dd, pd, rg, rb)
-    full = lax.all_gather(flat, ("dp", "fsdp"), axis=0, tiled=False).reshape(nd, nf, -1)
-    sizes = [v.size for v in shards]
-    parts, at = [], 0
-    for v, n in zip(shards, sizes):
-        parts.append(full[:, :, at:at + n].reshape((nd, nf) + v.shape))
-        at += n
-    ud_f = parts[0].transpose(0, 2, 1, 3).reshape(64, 128).astype(F32)
-    dd_f = parts[1].transpose(2, 0, 3, 1, 4).reshape(3, 32, 96).astype(F32)
-    pd_f = parts[2].transpose(2, 3, 0, 4, 1, 5).reshape(3, 2, 32, 32).astype(F32)
-    ug_f = parts[3][0].reshape(64).astype(F32)
-    ub_f = parts[4][0].reshape(32)
-    rg_f = parts[5][0].transpose(1, 2, 0, 3).reshape(3, 3, 32).astype(F32)
-    rb_f = parts[6][0].transpose(1, 2, 0, 3).reshape(3, 3, 32)
-    un = jnp.sqrt(jnp.sum(ud_f * ud_f, axis=1, keepdims=True))
-    dn = jnp.sqrt(jnp.sum(dd_f * dd_f, axis=2, keepdims=True))
-    pn = jnp.sqrt(jnp.sum(pd_f * pd_f, axis=3, keepdims=True))
-    us, ds, ps = ug_f[:, None], rg_f[:, 0, :, None], rg_f[:, 1:, :, None]
-    wts = prep((us * ud_f / un).astype(BF), (ds * dd_f / dn).astype(BF), (ps * pd_f / pn).astype(BF), ub_f, rb_f)
-    out, sg, gu, gd, gp, gb = main_call(NC, signal, segments, cotangent, wts)
-    gu = gu.reshape(4, 32, 64)[jnp.array([3, 0, 1, 2])].transpose(2, 1, 0).reshape(64, 128)
-    gd = gd.reshape(3, 3, 32, 32)[:, ::-1].transpose(0, 2, 1, 3).reshape(3, 32, 96)
-    gp = gp.reshape(3, 2, 32, 32).transpose(0, 1, 3, 2)
-    gb = gb.sum(-1)
-    gud, gug = norm_backward(ud_f, us, un, gu)
-    gdd, gdg = norm_backward(dd_f, ds, dn, gd)
-    gpd, gpg = norm_backward(pd_f, ps, pn, gp)
-    grg = jnp.concatenate([gdg[:, None], gpg], axis=1)
-    grb = jnp.stack([gb[:, 0], gb[:, 1], gb[:, 1]], axis=1)
-    a, b = ud.shape
-    m0 = gud.reshape(nd, a, nf, b).transpose(0, 2, 1, 3).reshape(nd, nf, -1)
-    a, b = dd.shape[1:]
-    m1 = gdd.reshape(3, nd, a, nf, b).transpose(1, 3, 0, 2, 4).reshape(nd, nf, -1)
-    a, b = pd.shape[2:]
-    m2 = gpd.reshape(3, 2, nd, a, nf, b).transpose(2, 4, 0, 1, 3, 5).reshape(nd, nf, -1)
-    sm = [gug.reshape(nf, -1), gb[0, 2].reshape(nf, -1), grg.reshape(9, nf, -1).transpose(1, 0, 2).reshape(nf, -1),
-          grb.reshape(9, nf, -1).transpose(1, 0, 2).reshape(nf, -1)]
-    sm = jnp.broadcast_to(jnp.concatenate(sm, axis=1)[None], (nd, nf, sum(v.shape[1] for v in sm)))
-    msg = jnp.concatenate([m0, m1, m2, sm], axis=2).reshape(nd * nf, -1)
-    tot = lax.psum_scatter(msg, ("dp", "fsdp"), scatter_dimension=0, tiled=True)[0]
-    res, at = [], 0
-    for v, n in zip(shards, sizes):
-        res.append(tot[at:at + n].reshape(v.shape))
-        at += n
-    return out, sg, res[0], res[3], res[4], res[1], res[2], res[5], res[6]
+MESH = pl.DeviceIdType.MESH
+
+
+def peer(lay, k):
+    me = lax.axis_index("dp") * lay.nf + lax.axis_index("fsdp")
+    t = lax.rem(me + k, lay.n)
+    return me, t, {"dp": t // lay.nf, "fsdp": lax.rem(t, lay.nf)}
+
+
+def greet(lay):
+    barrier = pltpu.get_barrier_semaphore()
+
+    def hello(k, c):
+        _, _, dev = peer(lay, k)
+        pl.semaphore_signal(barrier, inc=1, device_id=dev, device_id_type=MESH)
+        return c
+
+    lax.fori_loop(1, lay.n, hello, 0)
+    return barrier
+
+
+def exchange(lay, source, recv, send_sem, recv_sem):
+    def copy(k):
+        me, t, dev = peer(lay, k)
+        return pltpu.make_async_remote_copy(
+            src_ref=source(t), dst_ref=recv.at[me], send_sem=send_sem.at[k], recv_sem=recv_sem.at[k],
+            device_id=dev, device_id_type=MESH)
+
+    def start(k, c):
+        copy(k).start()
+        return c
+
+    def finish(k, c):
+        copy(k).wait()
+        return c
+
+    lax.fori_loop(1, lay.n, start, 0)
+    lax.fori_loop(1, lay.n, finish, 0)
+
+
+def gather_kernel(lay, ud, dd, pd, ug, ub, rg, rb, out, acc, msg, recv, send_sem, recv_sem):
+    barrier = greet(lay)
+    acc[...] = jnp.zeros_like(acc)
+    for p, o in enumerate(lay.u):
+        acc[:, o:o + lay.wu] = ud[8 * p:8 * p + 8].astype(F32)
+    for b in range(3):
+        acc[:, lay.d[b]:lay.d[b] + lay.wd] = dd[b].astype(F32)
+        for j in range(2):
+            o = lay.p[2 * b + j]
+            acc[:, o:o + lay.wp] = pd[b, j].astype(F32)
+        o = lay.r[b]
+        acc[0:3, o:o + lay.wr] = rg[b].astype(F32)
+        acc[3:6, o:o + lay.wr] = rb[b].astype(F32)
+    acc[0:1, lay.g:lay.g + lay.wg] = ug[...].astype(F32)
+    acc[1:2, lay.g:lay.g + lay.wr] = ub[...].astype(F32)
+    msg[...] = acc[...].astype(BF)
+    me = peer(lay, 0)[0]
+    recv[me] = acc[...].astype(BF)
+    pl.semaphore_wait(barrier, lay.n - 1)
+    exchange(lay, lambda t: msg, recv, send_sem, recv_sem)
+    out[...] = recv[...]
+
+
+def scatter_kernel(lay, msgs, out, recv, send_sem, recv_sem):
+    barrier = greet(lay)
+    me = peer(lay, 0)[0]
+    recv[me] = msgs[me]
+    pl.semaphore_wait(barrier, lay.n - 1)
+    exchange(lay, lambda t: msgs.at[t], recv, send_sem, recv_sem)
+    out[...] = recv[...]
+
+
+def sum_kernel(lay, recv, gud, gug, gub, gdd, gpd, grg, grb):
+    t = recv[0].astype(F32)
+    for s in range(1, lay.n):
+        t = t + recv[s].astype(F32)
+    for p, o in enumerate(lay.u):
+        gud[8 * p:8 * p + 8] = t[:, o:o + lay.wu]
+    for b in range(3):
+        gdd[b] = t[:, lay.d[b]:lay.d[b] + lay.wd]
+        for j in range(2):
+            o = lay.p[2 * b + j]
+            gpd[b, j] = t[:, o:o + lay.wp]
+        o = lay.r[b]
+        grg[b] = t[0:3, o:o + lay.wr]
+        grb[b] = t[3:6, o:o + lay.wr]
+    gug[...] = t[0:1, lay.g:lay.g + lay.wg]
+    gub[...] = t[1:2, lay.g:lay.g + lay.wr]
+
+
+def per_device(lay, signal, segments, cotangent, ud, ug, ub, dd, pd, rg, rb):
+    V = pl.BlockSpec(memory_space=pltpu.VMEM)
+    tiles = jax.ShapeDtypeStruct((lay.n, 8, L), BF)
+    sems = [pltpu.SemaphoreType.DMA((lay.n,)), pltpu.SemaphoreType.DMA((lay.n,))]
+    table = pl.pallas_call(
+        functools.partial(gather_kernel, lay), name="gather_params", out_shape=tiles,
+        in_specs=[V] * 7, out_specs=V,
+        scratch_shapes=[pltpu.VMEM((8, L), F32), pltpu.VMEM((8, L), BF), pltpu.VMEM((lay.n, 8, L), BF)] + sems,
+        compiler_params=pltpu.CompilerParams(collective_id=0, has_side_effects=True),
+    )(ud, dd, pd, ug.reshape(1, -1), ub.reshape(1, -1), rg, rb)
+    out, sg, msgs = main_call(NC, lay, signal, segments, cotangent, table)
+    got = pl.pallas_call(
+        functools.partial(scatter_kernel, lay), name="scatter_grads", out_shape=tiles,
+        in_specs=[V], out_specs=V,
+        scratch_shapes=[pltpu.VMEM((lay.n, 8, L), BF)] + sems,
+        compiler_params=pltpu.CompilerParams(collective_id=1, has_side_effects=True),
+    )(msgs)
+    f = lambda *s: jax.ShapeDtypeStruct(s, F32)
+    gud, gug, gub, gdd, gpd, grg, grb = pl.pallas_call(
+        functools.partial(sum_kernel, lay), name="sum_grads",
+        out_shape=(f(*ud.shape), f(1, ug.shape[0]), f(1, ub.shape[0]), f(*dd.shape), f(*pd.shape), f(*rg.shape), f(*rb.shape)),
+        in_specs=[V], out_specs=(V,) * 7,
+    )(got)
+    return out, sg, gud, gug.reshape(-1), gub.reshape(-1), gdd, gpd, grg, grb
 
 
 NC = 4
 
 
 def solution(mesh):
-    nd, nf = mesh.shape["dp"], mesh.shape["fsdp"]
+    lay = Lay(mesh.shape["dp"], mesh.shape["fsdp"])
     return jax.shard_map(
-        functools.partial(per_device, nd, nf),
+        functools.partial(per_device, lay),
         mesh=mesh,
         in_specs=(
             P(("dp", "fsdp"), None, None),

time: 309 us -> 127 us (0.41)
  waiting for transfers between devices: 121 us -> 0 us
  blocking collectives: 42.5 us -> 0 us
  Pallas kernels: 91.7 us -> 122 us
  local copies, waits for them, and re-layouts: 27.2 us -> 2.84 us
  between operations: 14.5 us -> 0.68 us
  other arithmetic: 10.4 us -> 0.83 us
    unnamed x2 -> x0, waiting for transfers between devices: 121 us -> none
    unnamed x1 -> x0, blocking collectives: 42.5 us -> none
    pallas_call x1 -> x4, Pallas kernels: 91.7 us -> 122 us  [the longest x1 98.6 us: main_call(): pl.pallas_call(functools.partial(main_kernel, NC, packs, cpp, lay), name=...]
    reshape x22 -> x0, local copies, waits for them, and re-layouts: 8.54 us -> none  [the longest x5 3.23 us: pack_local(): v.reshape(-1)]
    slice x10 -> x0, local copies, waits for them, and re-layouts: 5.78 us -> none  [the longest x6 5.73 us: per_device(): res.append(tot[at:at + n].reshape(v.shape))]
    convert_element_type x23 -> x0, local copies, waits for them, and re-layouts: 3.37 us -> none  [the longest x2 0.73 us: per_device(): ug_f = parts[3][0].reshape(64).astype(F32)]
  transfers between devices with their start and end apart: 1 -> 0, of which waited for: 1 -> 0; matrix products, arithmetic and copies ran while one was open for 0% -> 0% of each run, Pallas kernels for 0% -> 0%
where the time goes in v2:
time: 127 us
  Pallas kernels  122 us (96%)
  local copies, waits for them, and re-layouts  2.84 us (2%)
    pallas_call x1, Pallas kernels, main_call(): pl.pallas_call(functools.partial(main_kernel, NC, packs, cpp, lay), name=...  98.6 us
    pallas_call x1, Pallas kernels, per_device(): pl.pallas_call(functools.partial(gather_kernel, lay), name='gather_params...  12.1 us
    pallas_call x1, Pallas kernels, per_device(): pl.pallas_call(functools.partial(scatter_kernel, lay), name='scatter_grad...  9.89 us
    unnamed x2, local copies, waits for them, and re-layouts  2.84 us

profile of v2, /device:TPU:0, one launch (start us, length us, event | category | flops | bytes accessed | tf_op | source)
XLA Modules:
  0.0 126.5 jit_solution(483658268557504937)
XLA Ops:
  0.7 1.4 %copy.19.pd = bf16[3,2,8,4]{3,2,1,0:T(8,128)(2,1)} copy(bf16[3,2,8,4]{2,3,1,0:T(4,128)(2,1)} %param.17) | data formatting | bytes 768 | tf_op args[7]
  2.1 12.1 %gather_params.1.recv = bf16[32,8,128]{2,1,0:T(8,128)(2,1)} custom-call(bf16[16,16]{1,0:T(8,128)(2,1)} %ud.1, bf16[3,8,12]{2,1,0:T(8,128)(2,1)} %dd.1, bf16[3,2,8,4]{3,2,1,0:T(8,128)(2,1)} %copy.19.pd, bf16[1,8]{1,0:T(2,128)(2,1)} %bitcast.4, bf16[1,4]{1,0:T(2,128)(2,1)} %bitcast.5, bf16[3,3,4]{2,1,0:T(4,128)(2,1)} %rg.1, bf16[3,3,4]{2,1,0:T(4,128)(2,1)} %rb.1), custom_call_target="tpu_custom_call" | custom-call | tf_op jit(solution)/shard_map/gather_params/pallas_call | solution.py:510
  14.2 0.1 iota_compare_fusion.1
  14.3 0.7 add_convert_fusion.perm_in
  15.0 98.6 %section.1 = (bf16[8,32,8192]{2,1,0:T(8,128)(2,1)}, bf16[8,64,4096]{2,1,0:T(8,128)(2,1)}, bf16[32,8,128]{2,1,0:T(8,128)(2,1)}) custom-call(bf16[8,64,4096]{2,1,0:T(8,128)(2,1)} %sig_h.1, s32[8,4096]{1,0:T(8,128)} %seg.1, bf16[8,32,8192]{2,1,0:T(8,128)(2,1)} %cot_h.1, bf16[32,8,128]{2,1,0:T(8,128)(2,1)} %gather_params.1.recv, ...), custom_call_target="tpu_custom_call" | custom-call | tf_op jit(solution)/shard_map/section/pallas_call | solution.py:401
  113.6 9.9 %scatter_grads.1.recv = bf16[32,8,128]{2,1,0:T(8,128)(2,1)} custom-call(bf16[32,8,128]{2,1,0:T(8,128)(2,1)} %get-tuple-element.21.msgs), custom_call_target="tpu_custom_call" | custom-call | tf_op jit(solution)/shard_map/scatter_grads/pallas_call | solution.py:517
  123.5 1.6 %sum_grads.1 = (f32[16,16]{1,0:T(8,128)}, f32[1,8]{1,0:T(1,128)}, f32[1,4]{1,0:T(1,128)}, f32[3,8,12]{2,1,0:T(8,128)}, f32[3,2,8,4]{3,2,1,0:T(8,128)}, /*index=5*/f32[3,3,4]{2,1,0:T(4,128)}, f32[3,3,4]{2,1,0:T(4,128)}) custom-call(bf16[32,8,128]{2,1,0:T(8,128)(2,1)} %scatter_grads.1.recv), custom_call_target="tpu_custom_call" | custom-call | tf_op jit(solution)/shard_map/sum_grads/pallas_call | solution.py:524
  125.1 1.4 %copy.20 = f32[3,2,8,4]{2,3,1,0:T(4,128)} copy(f32[3,2,8,4]{3,2,1,0:T(8,128)} %get-tuple-element.35) | data formatting | bytes 1536
  (1 shorter events, 0.0 us)

commit v3 on v2

--- a/solution.py
+++ b/solution.py
@@ -13,11 +13,38 @@
 def dot_nt(a,b):
     return lax.dot_general(a,b,(((1,),(1,)),((),())),preferred_element_type=F32)
 
-def act_pair(v):
-    th=jnp.tanh(0.5*v); a=0.6+0.4*th
-    return v*a, a+(0.2*v)*(1.0-th*th)
+def act_pair(h):
+    h=h.astype(F32)
+    v=h.astype(BF); w=(0.2*h).astype(BF)
+    c=lambda x: jnp.asarray(x,BF)
+    th=jnp.tanh(c(0.5)*v); t=c(3.0)+c(2.0)*th; q=c(1.0)-th*th
+    return w*t, t+v*q
 
 KINDS={-1:0,1:1,-2:2,2:3,-4:4,4:5,-5:6,5:7}
+
+NAMES=("V1","S","NTP","A","B2","B3","cz","D1","D2","G2f","D3","GD2f","O","U1","U2","F")
+
+
+def FULL(e):
+    V1,S,NTP,A,B2,B3,cz,D1,D2,G2f,D3,GD2f,O,U1,U2,F=[e[k] for k in NAMES]
+    cz(); NTP(0); S(0); S(1); S(2); NTP(1)
+    D1(2); V1(); A(0); A(1); D1(1)
+    D2(2); G2f(); A(2); B2(0); B2(1)
+    D1(0); D3(2); GD2f(); B2(2); B3(1); D2(1)
+    U1(); O(); B3(2); D3(1); D2(0); U2(); F()
+    NTP(2); D3(0)
+
+
+def FILL(e):
+    V1,S,NTP,A,B2,B3,cz,D1,D2,G2f,D3,GD2f,O,U1,U2,F=[e[k] for k in NAMES]
+    D1(1); D1(0); U1(); D2(1); D2(0); U2(); F(); D3(1); D3(0)
+
+
+def DRAIN(e):
+    V1,S,NTP,A,B2,B3,cz,D1,D2,G2f,D3,GD2f,O,U1,U2,F=[e[k] for k in NAMES]
+    NTP(0); S(0); S(1); S(2)
+    V1(); A(0); A(1); A(2); B2(0); B2(1); B2(2); NTP(1); NTP(2); B3(1); B3(2)
+
 
 class Lay:
     def __init__(self, nd, nf):
@@ -123,7 +150,7 @@
         if c.shape[0]==32: c=jnp.concatenate([c,jnp.zeros((32,L),F32)],axis=0)
         return jnp.where(lane==q,c,C)
     perm=tap_perm()
-    v=dot(dirs[0:64].astype(BF),perm); w=dU[...]; s=cols[0,0:64]; i=cols[1,0:64]
+    v=dot(dirs[0:64].astype(BF),perm); w=dU[...].T[:64]; s=cols[0,0:64]; i=cols[1,0:64]
     inner=rs(w*v)
     C=place(C,24,inner*i)
     g=s*(w-(inner*i*i)*v)
@@ -138,7 +165,8 @@
         C=place(C,8*b,inner*i)
         gd.append(s*(w-(inner*i*i)*v))
         r=160+32*b
-        tmp[3+b,:,:64]=dP[b]
+        m=jnp.concatenate([dP[b],jnp.zeros((64,L),F32)],axis=0).T
+        tmp[3+b]=m[:32]
         v=dirs[r:r+32]; w=tmp[3+b]; s=cols[0,r:r+32]; i=cols[1,r:r+32]
         p=w*v
         inner=jnp.where(lane32<32,rs(jnp.where(lane32<32,p,0.0)),rs(jnp.where(lane32<32,0.0,p)))
@@ -165,10 +193,10 @@
             msgs[d*nf+f]=x.astype(BF)
 
 
-def main_kernel(NC, packs, cpp, lay, sig_h, seg, cot_h, recv, perm_in, out_h, sg_h, msgs,
+def main_kernel(NC, packs, cpp, lay, sig_h, seg, cot_h, recv, out_h, sg_h, msgs,
                 sig, cot, outb, sgb, dU, dD, dP, dB, dirs, cols, tmp, bias, sem_in, sem_out):
     def body(masks, wu, wv, wd, wdb, pf, pt, perm, *rings):
-        perm[...]=perm_in[...]
+        make_perm(perm)
         main_body(NC,packs,cpp,lay,recv,sig_h,seg,cot_h,wu,wv,wd,wdb,pf,pt,bias,perm,out_h,sg_h,msgs,dU,dD,dP,dB,
                   sig,cot,outb,sgb,dirs,cols,tmp,sem_in,sem_out,masks,rings)
     pl.run_scoped(body,pltpu.VMEM((packs*cpp,8,16,L),BF),
@@ -252,146 +280,140 @@
         ok=(j>=0)&(j<NCOL)
         jc=clampj(j)
         return jnp.where(ok,jc//cpp,packs), jc%cpp
-    def st_V(base):
-        j=base-dl[8]
-        x=ld(GU,j-1,NC+2)
-        gu=x[:,L:L+W]
-        gt=jnp.concatenate([gu, shf(x[:32],1)*mask(1,j,32), shf(x[32:],-1)*mask(-1,j,32)],axis=0)
-        fi=ld(FIRST,j); df=ld(DFIRST,j)
-        y=dot(wv[...],gt)
-        yield
-        dU[...]+=dot_nt(fi,gt)
-        yield
-        sgv=(y*df.astype(F32)).astype(BF)
-        for k in range(NC):
-            p,c=po(j+k)
-            sgb[p,:,pl.ds(pl.multiple_of(c*L,L),L)]=sgv[:,k*L:(k+1)*L]
-    def st_B(base,b,si):
-        j=base-dl[si]
-        sE,sO=stack(GD[b],j,b)
-        g=ld(G[b],j); pre=ld(PRE[b],j); dh=ld(DH[b],j); act=ld(ACT[b],j); hid=ld(HID[b],j)
-        ddp=ld(DD[b-1],j) if b else None
-        A=per_phase(wdb[b],sE,sO)
-        S=per_phase(pt[b,32:],g[:32],g[32:])
-        yield
-        dD[b]+=dot_nt(sE,pre[:32])+dot_nt(sO,pre[32:])
-        yield
-        gf=dh.astype(F32)*A+S
-        gl=gf.astype(BF)
-        if b==0:
-            st(GU,j,gl); dB[0,2]+=rowsum(gf)
-        else:
-            st(G[b-1],j,gl)
-            ag=per_phase(pt[b-1,:32],gl[:32],gl[32:])
-        yield
-        dP[b]+=dot_nt(g[:32],jnp.concatenate([act[:32],hid[:32]],axis=0))+dot_nt(g[32:],jnp.concatenate([act[32:],hid[32:]],axis=0))
-        if b:
-            dB[b-1,1]+=rowsum(gf)
-            yield
-            gd=ddp.astype(F32)*ag
+    def cat0(*v): return jnp.concatenate(v,axis=0)
+    def step(order,i,_):
+        base=i*NC
+        X={}
+        jv=base-dl[8]; jb=[base-dl[7],base-dl[6],base-dl[5]]; jd=[base-dl[2],base-dl[3],base-dl[4]]; ju=base-dl[1]
+        def V1():
+            x=ld(GU,jv-1,NC+2)
+            gu=x[:,L:L+W]
+            gt=cat0(gu, shf(x[:32],1)*mask(1,jv,32), shf(x[32:],-1)*mask(-1,jv,32))
+            y=dot(wv[...],gt)
+            dU[:,:64]+=dot_nt(gt,ld(FIRST,jv))
+            sgv=((0.2*y)*ld(DFIRST,jv).astype(F32)).astype(BF)
+            for k in range(NC):
+                p,c=po(jv+k)
+                sgb[p,:,pl.ds(pl.multiple_of(c*L,L),L)]=sgv[:,k*L:(k+1)*L]
+        def S(b):
+            g=ld(G[b],jb[b])
+            X['S',b]=per_phase(pt[b,32:],g[:32],g[32:])
+        def NTP(b):
+            g=ld(G[b],jb[b]); act=ld(ACT[b],jb[b]); hid=ld(HID[b],jb[b])
+            dP[b,:,:32]+=dot_nt(cat0(act[:32],hid[:32]),g[:32])+dot_nt(cat0(act[32:],hid[32:]),g[32:])
+        def A(b):
+            sE,sO=stack(GD[b],jb[b],b)
+            X['A',b]=per_phase(wdb[b],sE,sO)
+            pre=ld(PRE[b],jb[b])
+            dD[b]+=dot_nt(sE,pre[:32])+dot_nt(sO,pre[32:])
+        def B2(b):
+            gf=ld(DH[b],jb[b]).astype(F32)*(0.2*X['A',b])+X['S',b]
+            gl=gf.astype(BF)
+            if b==0:
+                st(GU,jb[b],gl); dB[0,2]+=rowsum(gf)
+            else:
+                st(G[b-1],jb[b],gl); dB[b-1,1]+=rowsum(gf)
+                X['ag',b-1]=per_phase(pt[b-1,:32],gl[:32],gl[32:])
+        def B3(b):
+            gd=ld(DD[b-1],jb[b]).astype(F32)*(0.2*X['ag',b-1])
             dB[b-1,0]+=rowsum(gd)
-            st(GD[b-1],j,gd)
-    def st_D(base,b):
-        j=base-dl[2+b]
-        sE,sO=stack(PRE[b],j,b)
-        hid=ld(HID[b],j)
-        dil=per_phase(wd[b],sE,sO)
-        if b==2:
+            st(GD[b-1],jb[b],gd)
+        def cz():
             cs=[]
             for k in range(NC):
-                p,c=pc(j+k)
+                p,c=pc(jd[2]+k)
                 cs.append(cot[p,:,pl.ds(pl.multiple_of(c*2*L,2*L),2*L)])
-            cz=dot(jnp.concatenate(cs,axis=0),perm[1])
-        yield
-        yield
-        dil=dil+bcol(1+2*b)
-        act,dd=act_pair(dil)
-        act=act.astype(BF)
-        st(ACT[b],j,act)
-        h=per_phase(pf[b],jnp.concatenate([act[:32],hid[:32]],axis=0),jnp.concatenate([act[32:],hid[32:]],axis=0))
-        if b<2:
-            st(DD[b],j,dd)
-        else:
+            X['cz']=dot(cat0(*cs),perm[1])
+        def D1(b):
+            sE,sO=stack(PRE[b],jd[b],b)
+            X['dil',b]=per_phase(wd[b],sE,sO)
+        def D2(b):
+            act,dd=act_pair(X['dil',b]+bcol(1+2*b))
+            act=act.astype(BF)
+            st(ACT[b],jd[b],act)
+            if b<2: st(DD[b],jd[b],dd)
+            else: X['dd']=dd
+            hid=ld(HID[b],jd[b])
+            X['h',b]=per_phase(pf[b],cat0(act[:32],hid[:32]),cat0(act[32:],hid[32:]))
+        def G2f():
+            cz=X['cz']; j=jd[2]
             gE=jnp.concatenate([cz[k*32:(k+1)*32,:L] for k in range(NC)],axis=1)
             gO=jnp.concatenate([cz[k*32:(k+1)*32,L:] for k in range(NC)],axis=1)
-            gf=jnp.concatenate([gE,gO],axis=0)
+            gf=cat0(gE,gO)
             vk=[jnp.where((j+k>=0)&(j+k<NCOL),1.0,0.0) for k in range(NC)]
             gf=jnp.concatenate([gf[:,k*L:(k+1)*L]*vk[k] for k in range(NC)],axis=1)
             gl=gf.astype(BF)
             st(G2,j,gl)
             dB[2,1]+=rowsum(gf)
-            ag=per_phase(pt[2,:32],gl[:32],gl[32:])
-        yield
-        yield
-        h=h+bcol(2+2*b)
-        if b<2:
+            X['ag',2]=per_phase(pt[2,:32],gl[:32],gl[32:])
+        def D3(b):
+            h=X['h',b]+bcol(2+2*b)
+            if b<2:
+                pre,dh=act_pair(h)
+                st(PRE[b+1],jd[b],pre); st(HID[b+1],jd[b],h); st(DH[b+1],jd[b],dh)
+            else:
+                ho=h.astype(BF)
+                z=cat0(*[jnp.concatenate([ho[:32,k*L:(k+1)*L],ho[32:,k*L:(k+1)*L]],axis=1) for k in range(NC)])
+                X['z']=dot(z,perm[0])
+        def GD2f():
+            gd=X['dd'].astype(F32)*(0.2*X['ag',2])
+            dB[2,0]+=rowsum(gd)
+            st(GD2,jd[2],gd)
+        def O():
+            z=X['z'].astype(BF)
+            for k in range(NC):
+                p,c=po(jd[2]+k)
+                outb[p,:,pl.ds(pl.multiple_of(c*2*L,2*L),2*L)]=z[k*32:(k+1)*32]
+        def U1():
+            x=ld(FIRST,ju-1,NC+2)
+            f0=x[:,L:L+W]
+            fm=shf(x,-1)*mask(-1,ju,64); fp=shf(x,1)*mask(1,ju,64)
+            X['u']=cat0(dot(wu[0],cat0(f0,fm)),dot(wu[1],cat0(f0,fp)))
+        def U2():
+            h=X['u']+bcol(0)
             pre,dh=act_pair(h)
-            st(PRE[b+1],j,pre); st(HID[b+1],j,h); st(DH[b+1],j,dh)
-        else:
-            ho=h.astype(BF)
-            z=jnp.concatenate([jnp.concatenate([ho[:32,k*L:(k+1)*L],ho[32:,k*L:(k+1)*L]],axis=1) for k in range(NC)],axis=0)
-            z=dot(z,perm[0])
-            gd=dd*ag
-            dB[2,0]+=rowsum(gd)
-            st(GD2,j,gd)
-            yield
-            z=z.astype(BF)
+            st(PRE0,ju,pre); st(HID0,ju,h); st(DH0,ju,dh)
+        def F():
+            xs=[]
             for k in range(NC):
-                p,c=po(j+k)
-                outb[p,:,pl.ds(pl.multiple_of(c*2*L,2*L),2*L)]=z[k*32:(k+1)*32]
-    def st_U(base):
-        j=base-dl[1]
-        x=ld(FIRST,j-1,NC+2)
-        f0=x[:,L:L+W]
-        fm=shf(x,-1)*mask(-1,j,64); fp=shf(x,1)*mask(1,j,64)
-        h=jnp.concatenate([dot(wu[0],jnp.concatenate([f0,fm],axis=0)),dot(wu[1],jnp.concatenate([f0,fp],axis=0))],axis=0)
-        yield
-        yield
-        h=h+bcol(0)
-        pre,dh=act_pair(h)
-        st(PRE0,j,pre); st(HID0,j,h); st(DH0,j,dh)
-    def st_F(base):
-        j=base
-        xs=[]
-        for k in range(NC):
-            p,c=pc(j+k)
-            xs.append(sig[p,:,pl.ds(pl.multiple_of(c*L,L),L)])
-        x=jnp.concatenate(xs,axis=1)
-        yield
-        fv,dv=act_pair(x.astype(F32))
-        st(FIRST,j,fv); st(DFIRST,j,dv)
-    def step(i,_):
-        base=i*NC
-        gens=[st_V(base),st_D(base,2),st_B(base,0,7),st_B(base,1,6),st_D(base,1),st_B(base,2,5),st_D(base,0),st_U(base),st_F(base)]
-        while gens:
-            nxt=[]
-            for g in gens:
-                try: next(g); nxt.append(g)
-                except StopIteration: pass
-            gens=nxt
+                p,c=pc(base+k)
+                xs.append(sig[p,:,pl.ds(pl.multiple_of(c*L,L),L)])
+            fv,dv=act_pair(jnp.concatenate(xs,axis=1))
+            st(FIRST,base,fv); st(DFIRST,base,dv)
+        order(dict(locals()))
         return 0
+    lo=lambda d: -((NC-1-d)//NC)
+    hi=lambda d: (NCOL-1+d)//NC+1
+    first_full=lo(dl[4]); last_full=hi(dl[4]); total=hi(dl[8])
     ipp=cpp//NC
-    def outer(g,_):
-        for c in copies_in(g): c.wait()
-        lax.fori_loop(g*ipp,(g+1)*ipp,step,0)
-        @pl.when(g>=2)
+    done=(cpp-1+dl[8])//NC+1
+    for c in copies_in(0): c.wait()
+    lax.fori_loop(0,first_full,functools.partial(step,FILL),0)
+    def full(i,c):
+        @pl.when((lax.rem(i,ipp)==0)&(i<packs*ipp))
         def _():
-            for c in copies_out(g-2): c.start()
-        return 0
-    lax.fori_loop(0,packs,outer,0)
-    tot=packs*ipp-(-dl[8]//NC)
-    lax.fori_loop(packs*ipp,tot,step,0)
-    for p in (packs-2,packs-1):
+            for q in copies_in(lax.div(i,ipp)): q.wait()
+        @pl.when((lax.rem(i,ipp)==done%ipp)&(i>=done))
+        def _():
+            for q in copies_out(lax.div(i-done,ipp)): q.start()
+        return step(FULL,i,c)
+    lax.fori_loop(first_full,last_full,full,0)
+    started=[p for p in range(packs) if p*ipp+done<last_full]
+    for k in range(NC*(total-last_full)+2):
+        for r in (G2,GD2): rings[r][slot(NCOL+k)]=jnp.zeros((64,L),BF)
+    lax.fori_loop(last_full,total,functools.partial(step,DRAIN),0)
+    for p in range(len(started),packs):
         for c in copies_out(p): c.start()
     epilogue(lay,dU,dD,dP,dB,dirs,cols,tmp,msgs)
     for p in range(packs):
         for c in copies_out(p): c.wait()
 
-def make_perm():
-    r=jnp.arange(2*L)[:,None]; c=jnp.arange(2*L)[None,:]
-    tgt=jnp.where(r<L,2*r,2*(r-L)+1)
-    P=(tgt==c).astype(BF)
-    return jnp.stack([P,P.T])
+
+def make_perm(perm):
+    r=lax.broadcasted_iota(jnp.int32,(2*L,2*L),0); c=lax.broadcasted_iota(jnp.int32,(2*L,2*L),1)
+    to=lambda x: jnp.where(x<L,2*x,2*(x-L)+1)
+    perm[0]=(to(r)==c).astype(F32).astype(BF)
+    perm[1]=(to(c)==r).astype(F32).astype(BF)
 
 
 def main_call(NC, lay, signal, segments, cot, recv):
@@ -402,14 +424,14 @@
         functools.partial(main_kernel,NC,packs,cpp,lay),
         name="section",
         out_shape=(jax.ShapeDtypeStruct(cot.shape,BF),jax.ShapeDtypeStruct(signal.shape,BF),jax.ShapeDtypeStruct((lay.n,8,L),BF)),
-        in_specs=[A,V,A,V,V], out_specs=(A,A,V),
+        in_specs=[A,V,A,V], out_specs=(A,A,V),
         scratch_shapes=[pltpu.VMEM(signal.shape,BF),pltpu.VMEM(cot.shape,BF),
             pltpu.VMEM((packs+1,32,2*T),BF),pltpu.VMEM((packs+1,64,T),BF),
-            pltpu.VMEM((64,L),F32),pltpu.VMEM((3,96,32),F32),pltpu.VMEM((3,32,64),F32),pltpu.VMEM((3,3,32,L),F32),
+            pltpu.VMEM((L,L),F32),pltpu.VMEM((3,96,32),F32),pltpu.VMEM((3,64,L),F32),pltpu.VMEM((3,3,32,L),F32),
             pltpu.VMEM((256,L),F32),pltpu.VMEM((2,256,L),F32),pltpu.VMEM((6,32,L),F32),pltpu.VMEM((7,32,L),F32),
             pltpu.SemaphoreType.DMA((2,packs)),pltpu.SemaphoreType.DMA((2,packs))],
-        compiler_params=pltpu.CompilerParams(vmem_limit_bytes=63<<20),
-    )(signal,segments,cot,recv,make_perm())
+        compiler_params=pltpu.CompilerParams(vmem_limit_bytes=54<<20),
+    )(signal,segments,cot,recv)
 
 from jax.sharding import PartitionSpec as P
 
@@ -453,24 +475,26 @@
     lax.fori_loop(1, lay.n, finish, 0)
 
 
-def gather_kernel(lay, ud, dd, pd, ug, ub, rg, rb, out, acc, msg, recv, send_sem, recv_sem):
+def gather_kernel(lay, ud, dd, pd, ug, ub, rg, rb, out, acc, sq, msg, recv, send_sem, recv_sem):
     barrier = greet(lay)
     acc[...] = jnp.zeros_like(acc)
+    sq[...] = jnp.zeros_like(sq)
     for p, o in enumerate(lay.u):
         acc[:, o:o + lay.wu] = ud[8 * p:8 * p + 8].astype(F32)
     for b in range(3):
         acc[:, lay.d[b]:lay.d[b] + lay.wd] = dd[b].astype(F32)
         for j in range(2):
-            o = lay.p[2 * b + j]
-            acc[:, o:o + lay.wp] = pd[b, j].astype(F32)
+            o = (2 * b + j) * lay.wp
+            sq[o:o + lay.wp, 0:8] = pd[b, j].astype(F32)
         o = lay.r[b]
         acc[0:3, o:o + lay.wr] = rg[b].astype(F32)
         acc[3:6, o:o + lay.wr] = rb[b].astype(F32)
     acc[0:1, lay.g:lay.g + lay.wg] = ug[...].astype(F32)
     acc[1:2, lay.g:lay.g + lay.wr] = ub[...].astype(F32)
-    msg[...] = acc[...].astype(BF)
+    full = put(acc[...], sq[...].T[:8], 0, lay.p[0], 6 * lay.wp).astype(BF)
+    msg[...] = full
     me = peer(lay, 0)[0]
-    recv[me] = acc[...].astype(BF)
+    recv[me] = full
     pl.semaphore_wait(barrier, lay.n - 1)
     exchange(lay, lambda t: msg, recv, send_sem, recv_sem)
     out[...] = recv[...]
@@ -489,13 +513,14 @@
     t = recv[0].astype(F32)
     for s in range(1, lay.n):
         t = t + recv[s].astype(F32)
+    m = jnp.concatenate([move(t, lay.p[0], 0), jnp.zeros((L - 8, L), F32)], axis=0).T
     for p, o in enumerate(lay.u):
         gud[8 * p:8 * p + 8] = t[:, o:o + lay.wu]
     for b in range(3):
         gdd[b] = t[:, lay.d[b]:lay.d[b] + lay.wd]
         for j in range(2):
-            o = lay.p[2 * b + j]
-            gpd[b, j] = t[:, o:o + lay.wp]
+            o = (2 * b + j) * lay.wp
+            gpd[b, j] = m[o:o + lay.wp, 0:8]
         o = lay.r[b]
         grg[b] = t[0:3, o:o + lay.wr]
         grb[b] = t[3:6, o:o + lay.wr]
@@ -510,9 +535,9 @@
     table = pl.pallas_call(
         functools.partial(gather_kernel, lay), name="gather_params", out_shape=tiles,
         in_specs=[V] * 7, out_specs=V,
-        scratch_shapes=[pltpu.VMEM((8, L), F32), pltpu.VMEM((8, L), BF), pltpu.VMEM((lay.n, 8, L), BF)] + sems,
+        scratch_shapes=[pltpu.VMEM((8, L), F32), pltpu.VMEM((L, L), F32), pltpu.VMEM((8, L), BF), pltpu.VMEM((lay.n, 8, L), BF)] + sems,
         compiler_params=pltpu.CompilerParams(collective_id=0, has_side_effects=True),
-    )(ud, dd, pd, ug.reshape(1, -1), ub.reshape(1, -1), rg, rb)
+    )(ud, dd, pd.transpose(0, 1, 3, 2), ug.reshape(1, -1), ub.reshape(1, -1), rg, rb)
     out, sg, msgs = main_call(NC, lay, signal, segments, cotangent, table)
     got = pl.pallas_call(
         functools.partial(scatter_kernel, lay), name="scatter_grads", out_shape=tiles,
@@ -523,10 +548,10 @@
     f = lambda *s: jax.ShapeDtypeStruct(s, F32)
     gud, gug, gub, gdd, gpd, grg, grb = pl.pallas_call(
         functools.partial(sum_kernel, lay), name="sum_grads",
-        out_shape=(f(*ud.shape), f(1, ug.shape[0]), f(1, ub.shape[0]), f(*dd.shape), f(*pd.shape), f(*rg.shape), f(*rb.shape)),
+        out_shape=(f(*ud.shape), f(1, ug.shape[0]), f(1, ub.shape[0]), f(*dd.shape), f(3, 2, pd.shape[3], pd.shape[2]), f(*rg.shape), f(*rb.shape)),
         in_specs=[V], out_specs=(V,) * 7,
     )(got)
-    return out, sg, gud, gug.reshape(-1), gub.reshape(-1), gdd, gpd, grg, grb
+    return out, sg, gud, gug.reshape(-1), gub.reshape(-1), gdd, gpd.transpose(0, 1, 3, 2), grg, grb
 
 
 NC = 4

time: 127 us -> 104 us (0.82)
  Pallas kernels: 122 us -> 103 us
  local copies, waits for them, and re-layouts: 2.84 us -> 0 us
    pallas_call x1, Pallas kernels: 98.6 us -> 79.7 us  [main_call(): pl.pallas_call(functools.partial(main_kernel, NC, packs, cpp, lay), name=...]
    unnamed x2 -> x0, local copies, waits for them, and re-layouts: 2.84 us -> none
where the time goes in v3:
time: 104 us
  Pallas kernels  103 us (99%)
    pallas_call x1, Pallas kernels, main_call(): pl.pallas_call(functools.partial(main_kernel, NC, packs, cpp, lay), name=...  79.7 us
    pallas_call x1, Pallas kernels, per_device(): pl.pallas_call(functools.partial(gather_kernel, lay), name='gather_params...  12.1 us
    pallas_call x1, Pallas kernels, per_device(): pl.pallas_call(functools.partial(scatter_kernel, lay), name='scatter_grad...  9.89 us

profile of v3, /device:TPU:0, one launch (start us, length us, event | category | flops | bytes accessed | tf_op | source)
XLA Modules:
  0.0 103.9 jit_solution(747023857522697122)
XLA Ops:
  0.6 12.1 %gather_params.1.recv = bf16[32,8,128]{2,1,0:T(8,128)(2,1)} custom-call(bf16[16,16]{1,0:T(8,128)(2,1)} %ud.1, bf16[3,8,12]{2,1,0:T(8,128)(2,1)} %dd.1, bf16[3,2,4,8]{3,2,1,0:T(4,128)(2,1)} %bitcast.6, bf16[1,8]{1,0:T(2,128)(2,1)} %bitcast.7, bf16[1,4]{1,0:T(2,128)(2,1)} %bitcast.8, bf16[3,3,4]{2,1,0:T(4,128)(2,1)} %rg.1, bf16[3,3,4]{2,1,0:T(4,128)(2,1)} %rb.1), custom_call_target="tpu_custom_call" | custom-call | tf_op jit(solution)/shard_map/gather_params/pallas_call | solution.py:535
  12.7 79.7 %section.1 = (bf16[8,32,8192]{2,1,0:T(8,128)(2,1)}, bf16[8,64,4096]{2,1,0:T(8,128)(2,1)}, bf16[32,8,128]{2,1,0:T(8,128)(2,1)}) custom-call(bf16[8,64,4096]{2,1,0:T(8,128)(2,1)} %sig_h.1, s32[8,4096]{1,0:T(8,128)} %seg.1, bf16[8,32,8192]{2,1,0:T(8,128)(2,1)} %cot_h.1, bf16[32,8,128]{2,1,0:T(8,128)(2,1)} %gather_params.1.recv), custom_call_target="tpu_custom_call" | custom-call | tf_op jit(solution)/shard_map/section/pallas_call | solution.py:423
  92.4 9.9 %scatter_grads.1.recv = bf16[32,8,128]{2,1,0:T(8,128)(2,1)} custom-call(bf16[32,8,128]{2,1,0:T(8,128)(2,1)} %get-tuple-element.21.msgs), custom_call_target="tpu_custom_call" | custom-call | tf_op jit(solution)/shard_map/scatter_grads/pallas_call | solution.py:542
  102.3 1.6 %sum_grads.1 = (f32[16,16]{1,0:T(8,128)}, f32[1,8]{1,0:T(1,128)}, f32[1,4]{1,0:T(1,128)}, f32[3,8,12]{2,1,0:T(8,128)}, f32[3,2,4,8]{3,2,1,0:T(4,128)}, /*index=5*/f32[3,3,4]{2,1,0:T(4,128)}, f32[3,3,4]{2,1,0:T(4,128)}) custom-call(bf16[32,8,128]{2,1,0:T(8,128)(2,1)} %scatter_grads.1.recv), custom_call_target="tpu_custom_call" | custom-call | tf_op jit(solution)/shard_map/sum_grads/pallas_call | solution.py:549

commit v4 on v3

v4 whole, which is shorter than its diff:
```python
import functools
import jax, jax.numpy as jnp
from jax import lax
from jax.experimental import pallas as pl
from jax.experimental.pallas import tpu as pltpu

BF=jnp.bfloat16; F32=jnp.float32
L=128

def dot(a,b):
    return jnp.dot(a,b,preferred_element_type=F32)
def dot_nt(a,b):
    return lax.dot_general(a,b,(((1,),(1,)),((),())),preferred_element_type=F32)

def act_pair(h):
    h=h.astype(F32)
    v=h.astype(BF); w=(0.2*h).astype(BF)
    c=lambda x: jnp.asarray(x,BF)
    th=jnp.tanh(c(0.5)*v); t=c(3.0)+c(2.0)*th; q=c(1.0)-th*th
    return w*t, t+v*q

KINDS={-1:0,1:1,-2:2,2:3,-4:4,4:5,-5:6,5:7}

NAMES=("V1","NT","A","B2","AG","PW","PA","B3","D1","D2","G2f","D3","GD2f","O","U1","U2","F")


def FULL(e):
    V1,NT,A,B2,AG,PW,PA,B3,D1,D2,G2f,D3,GD2f,O,U1,U2,F=[e[k] for k in NAMES]
    NT(2); NT(1); D1(2); A(2); G2f(); D1(1); D2(2); PA(2)
    D2(1); B2(2); A(0); A(1); D3(2); D1(0); V1(); PA(1)
    O(); D3(1); B2(1); B2(0); B3(2); NT(0); D2(0); PA(0)
    U1(); GD2f(); U2(); B3(1); D3(0); F()


def lags(NC):
    out=[0]
    for k in range(8):
        d=out[-1]+NC+1
        out.append(-(-d//NC)*NC if k in (3,7) else d)
    return out


def ring_sizes(NC):
    F,U,D0,D1,D2,B2,B1,B0,V=range(9)
    life=[(F,V),(F,V),(U,B0),(D0,B1),(D1,B2),(U,B0),(D0,B1),(D1,B2),(U,B0),(D0,B1),(D1,B2),
          (D0,B0),(D1,B1),(D2,B2),(D0,B1),(D1,B2),(D2,B2),(B2,B1),(B1,B0),(B1,B0),(B2,B1),(D2,B2),(D2,V)]
    out=[]; lag=lags(NC)
    for w,r in life:
        need=lag[r]-lag[w]+NC+2
        out.append(max(8,1<<(need-1).bit_length()))
    return out


UN=2
VMEM=28


class Lay:
    def __init__(self, nd, nf):
        self.nd, self.nf, self.n = nd, nf, nd * nf
        self.wu, self.wd, self.wp, self.wr, self.wg = 128 // nf, 96 // nf, 32 // nf, 32 // nf, 64 // nf
        self.pu = 64 // nd // 8
        at = 0
        self.u = []
        for _ in range(self.pu):
            self.u.append(at)
            at += self.wu
        self.d = []
        for _ in range(3):
            self.d.append(at)
            at += self.wd
        self.p = []
        for _ in range(6):
            self.p.append(at)
            at += self.wp
        self.r = []
        for _ in range(3):
            self.r.append(at)
            at += self.wr
        self.g = at
        assert at + self.wg <= 128


def lane8(): return lax.broadcasted_iota(jnp.int32,(8,L),1)


def move(x, frm, to):
    k=(to-frm)%L
    return x if k==0 else pltpu.roll(x,k,1)


def put(acc, x, frm, to, w):
    lane=lane8()
    return jnp.where((lane>=to)&(lane<to+w),move(x,frm,to),acc)


def tap_perm():
    r=lax.broadcasted_iota(jnp.int32,(L,L),0); c=lax.broadcasted_iota(jnp.int32,(L,L),1)
    pos=((r&3)+3)&3
    return (c==pos*32+(r>>2)).astype(F32).astype(BF)


def square(x):
    return jnp.concatenate([x,jnp.zeros((L-x.shape[0],L),F32)],axis=0) if x.shape[0]<L else x


def prologue(lay, recv, wu, wv, wd, wdb, pa, bias, dirs, cols):
    nd,nf=lay.nd,lay.nf
    z=jnp.zeros((8,L),F32)
    lane=lane8()
    def pick(x, at, w, acc):
        at=at%L
        return jnp.where((lane>=at)&(lane<at+w),x,acc)
    def gather(i, o, w, count):
        acc=[z]*count
        for f in range(nf):
            x=move(recv[i*nf+f].astype(F32),o,f*w)
            acc=[pick(x,(f+q)*w,w,y) for q,y in enumerate(acc)]
        return acc
    ud=jnp.concatenate([move(x,p*lay.wu,0) for i in range(nd) for p,x in enumerate(gather(i,lay.u[0],lay.wu,lay.pu))],axis=0)
    dd=[[] for _ in range(3)]; pd=[[] for _ in range(3)]
    for i in range(nd):
        x=gather(i,lay.d[0],lay.wd,3); y=gather(i,lay.p[0],lay.wp,6)
        for b in range(3):
            dd[b].append(move(x[b],b*lay.wd,0))
            pd[b].append(move(y[2*b],2*b*lay.wp,0)+move(y[2*b+1],(2*b+1)*lay.wp,32))
    dd=[jnp.concatenate(x,axis=0) for x in dd]; pd=[jnp.concatenate(x,axis=0) for x in pd]
    sm=[move(x,b*lay.wr,0) for b,x in enumerate(gather(0,lay.r[0],lay.wr,3))]+gather(0,lay.g,lay.wg,1)+gather(0,lay.g,lay.wr,1)
    st=square(jnp.concatenate(sm,axis=0)).T
    def col(q,rows): return jnp.broadcast_to(st[:rows,q:q+1],(rows,L))
    def norm(x): return jnp.broadcast_to(jnp.sqrt(jnp.sum(x*x,axis=1,keepdims=True)),x.shape)
    n=norm(ud); g=col(24,64)
    dirs[0:64]=ud; cols[0,0:64]=g/n; cols[1,0:64]=1.0/n
    w=dot((g*ud/n).astype(BF),tap_perm())
    wv[...]=w.astype(BF)
    m=jnp.concatenate([w,pltpu.roll(w,64,1)],axis=0).T
    lane=lax.broadcasted_iota(jnp.int32,(32,L),1)
    z32=jnp.zeros((32,L),F32)
    def left(x): return jnp.where(lane<64,x,0.0)
    x=jnp.concatenate([jnp.concatenate([m[:32],z32],axis=1),
                       jnp.concatenate([left(m[32:64]),left(pltpu.roll(m[32:64],64,1))],axis=1)],axis=0)
    wu[...]=x[:,:192].astype(BF)
    bias[0]=col(33,32)
    for b in range(3):
        r=64+32*b
        x=dd[b]; n=norm(x); g=col(8*b,32)
        dirs[r:r+32]=x; cols[0,r:r+32]=g/n; cols[1,r:r+32]=1.0/n
        w=(g*x/n).astype(BF).astype(F32)
        wd[b]=w[:,:96].astype(BF)
        m=square(jnp.concatenate([pltpu.roll(w,64,1),pltpu.roll(w,96,1),w],axis=0)).T
        back=m[:32]
        r=160+32*b
        x=pd[b]
        n=jnp.where(lane<32,norm(jnp.where(lane<32,x,0.0)),norm(jnp.where(lane<32,0.0,x)))
        g=jnp.where(lane<32,col(8*b+1,32),col(8*b+2,32))
        dirs[r:r+32]=x; cols[0,r:r+32]=g/n; cols[1,r:r+32]=1.0/n
        w=(g*x/n).astype(BF)
        w=w.astype(F32)
        m=square(w).T
        wide=jnp.where(lane<32,m[:64][32:],0.0)
        wdb[b]=jnp.concatenate([back,pltpu.roll(wide,96,1)],axis=0).astype(BF)
        wide=jnp.where(lane<32,m[:32],0.0)
        pa[b]=jnp.concatenate([w,pltpu.roll(wide,64,1)],axis=0)[:,:96].astype(BF)
        bias[1+2*b]=col(8*b+3,32)
        bias[2+2*b]=col(8*b+4,32)+col(8*b+5,32)


def epilogue(lay, dU, dN, dB, dirs, cols, tmp, msgs):
    nd,nf=lay.nd,lay.nf
    def rs(x): return jnp.sum(x,axis=1,keepdims=True)
    lane=lax.broadcasted_iota(jnp.int32,(64,L),1); lane32=lane[:32]
    C=jnp.zeros((64,L),F32)
    def place(C,q,c):
        c=jnp.broadcast_to(c,(c.shape[0],L))
        if c.shape[0]==32: c=jnp.concatenate([c,jnp.zeros((32,L),F32)],axis=0)
        return jnp.where(lane==q,c,C)
    perm=tap_perm()
    v=dot(dirs[0:64].astype(BF),perm); w=dU[...].T[:64]; s=cols[0,0:64]; i=cols[1,0:64]
    inner=rs(w*v)
    C=place(C,24,inner*i)
    g=s*(w-(inner*i*i)*v)
    gu=dot_nt(g.astype(BF),perm)
    gd=[];gp=[]
    tmp[...]=jnp.zeros_like(tmp)
    for b in range(3):
        r=64+32*b
        for t in range(3): tmp[b,:,t*32:t*32+32]=dN[b,(2-t)*32:(3-t)*32,:32]
        v=dirs[r:r+32]; w=tmp[b]; s=cols[0,r:r+32]; i=cols[1,r:r+32]
        inner=rs(w*v)
        C=place(C,8*b,inner*i)
        gd.append(s*(w-(inner*i*i)*v))
        r=160+32*b
        tmp[3+b]=square(dN[b,96:160]).T[:32]
        v=dirs[r:r+32]; w=tmp[3+b]; s=cols[0,r:r+32]; i=cols[1,r:r+32]
        p=w*v
        inner=jnp.where(lane32<32,rs(jnp.where(lane32<32,p,0.0)),rs(jnp.where(lane32<32,0.0,p)))
        C=place(C,8*b+1,inner[:,:1]*i[:,:1])
        C=place(C,8*b+2,inner[:,32:33]*i[:,32:33])
        gp.append(s*(w-(inner*i*i)*v))
        C=place(C,8*b+3,rs(dB[b,0]))
        o=rs(dB[b,1])
        C=place(C,8*b+4,o); C=place(C,8*b+5,o)
    C=place(C,33,rs(dB[0,2]))
    S=square(C).T
    lane=lane8(); row=lax.broadcasted_iota(jnp.int32,(8,L),0)
    def join(xs, f, w, o):
        acc=xs[0]
        for q,x in enumerate(xs[1:],1):
            at=(f+q)*w%L
            acc=jnp.where((lane>=at)&(lane<at+w),x,acc)
        return move(acc,f*w,o)
    def upto(at, x, y): return jnp.where(lane<at,x,y)
    us=[[move(gu[(d*lay.pu+p)*8:(d*lay.pu+p)*8+8],0,p*lay.wu) for p in range(lay.pu)] for d in range(nd)]
    ds=[[move(gd[b][8*d:8*d+8],0,b*lay.wd) for b in range(3)] for d in range(nd)]
    ps=[[move(gp[q//2][8*d:8*d+8],32*(q%2),q*lay.wp) for q in range(6)] for d in range(nd)]
    rs_=[move(S[8*b:8*b+8],0,b*lay.wr) for b in range(3)]
    for f in range(nf):
        g=jnp.where(row==1,move(S[32:40],f*lay.wr,lay.g),move(S[24:32],f*lay.wg,lay.g))
        sm=upto(lay.g,join(rs_,f,lay.wr,lay.r[0]),jnp.where(lane<lay.g+lay.wg,g,0.0))
        for d in range(nd):
            x=upto(lay.d[0],join(us[d],f,lay.wu,lay.u[0]),
              upto(lay.p[0],join(ds[d],f,lay.wd,lay.d[0]),
              upto(lay.r[0],join(ps[d],f,lay.wp,lay.p[0]),sm)))
            msgs[d*nf+f]=x.astype(BF)


def make_masks(seg, masks, cpp):
    T=cpp*L
    s=seg[...]
    pos=lax.broadcasted_iota(jnp.int32,s.shape,1)
    for k,kind in KINDS.items():
        r=pltpu.roll(s,(-k)%T,1)
        m=((r==s)&(pos+k>=0)&(pos+k<T)).astype(F32)
        for p in range(s.shape[0]):
            mp=jnp.broadcast_to(m[p:p+1,:],(16,T)).astype(BF)
            for c in range(cpp): masks[p*cpp+c,kind]=mp[:,c*L:(c+1)*L]


def main_kernel(NC, packs, cpp, lay, sig, masks, cot, recv, out_h, sg_h, dU, dN, dB, dirs, cols,
                outb, sgb, bias, sem_out):
    def body(wu, wv, wd, wdb, pa, perm, *rings):
        make_perm(perm)
        main_body(NC,packs,cpp,lay,recv,wu,wv,wd,wdb,pa,bias,perm,out_h,sg_h,dU,dN,dB,
                  sig,cot,outb,sgb,dirs,cols,sem_out,masks,rings)
    pl.run_scoped(body,pltpu.VMEM((64,192),BF),pltpu.VMEM((64,L),BF),pltpu.VMEM((3,32,96),BF),pltpu.VMEM((3,64,L),BF),
                  pltpu.VMEM((3,64,96),BF),pltpu.VMEM((2*L,2*L),BF),
                  *[pltpu.VMEM((r,64,L),BF) for r in ring_sizes(NC)])


def main_body(NC, packs, cpp, lay, recv, wu, wv, wd, wdb, pa, bias, perm,
              out_h, sg_h, dU, dN, dB, sig, cot, outb, sgb, dirs, cols, sem_out, masks, rings):
    NCOL=packs*cpp
    (FIRST,DFIRST,PRE0,PRE1,PRE2,HID0,HID1,HID2,DH0,DH1,DH2,ACT0,ACT1,ACT2,DD0,DD1,G2,G1,G0,GD0,GD1,GD2,GU)=range(23)
    PRE=(PRE0,PRE1,PRE2);HID=(HID0,HID1,HID2);DH=(DH0,DH1,DH2);ACT=(ACT0,ACT1,ACT2);DD=(DD0,DD1);GD=(GD0,GD1,GD2);G=(G0,G1,G2)
    dl=lags(NC)
    sizes=ring_sizes(NC)
    assert cpp%NC==0 and dl[4]%NC==0 and dl[8]%NC==0
    def copy_out_y(p): return pltpu.make_async_copy(outb.at[p],out_h.at[p],sem_out.at[0,p])
    def copy_out_x(p): return pltpu.make_async_copy(sgb.at[p],sg_h.at[p],sem_out.at[1,p])
    def copies_out(p): return copy_out_y(p),copy_out_x(p)
    dU[...]=jnp.zeros_like(dU); dN[...]=jnp.zeros_like(dN); dB[...]=jnp.zeros_like(dB)
    for r,q in zip(sizes,rings):
        n=min(r,dl[8]-dl[4]+4)
        q[pl.ds(r-n,n)]=jnp.zeros((n,64,L),BF)
    prologue(lay,recv,wu,wv,wd,wdb,pa,bias,dirs,cols)
    def slot(r,j): return j & (sizes[r]-1)
    def ld(r,j0,n):
        return jnp.concatenate([rings[r][slot(r,j0+k)] for k in range(n)],axis=1) if n>1 else rings[r][slot(r,j0)]
    def st(r,j0,v):
        v=v.astype(BF)
        for k in range(v.shape[1]//L): rings[r][slot(r,j0+k)]=v[:,k*L:(k+1)*L]
    def clampj(j): return min(max(j,0),NCOL-1) if isinstance(j,int) else jnp.clip(j,0,NCOL-1)
    def mult(x): return x if isinstance(x,int) else pl.multiple_of(x,NC*L)
    def cat0(*v): return jnp.concatenate(v,axis=0)
    def mask(kind,j0,rows,n):
        cols=[]
        for k in range(n):
            m=masks[clampj(j0+k),KINDS[kind]]
            cols.append(jnp.concatenate([m]*(rows//16),axis=0))
        return jnp.concatenate(cols,axis=1)
    def shf(x,k):
        W=x.shape[1]-2*L
        if k>0: return pltpu.roll(x[:,L:],W+L-k,1)[:,:W]
        return pltpu.roll(x[:,:W+L],-k,1)[:,L:]
    def stack(r,j0,n,b):
        x=ld(r,j0-1,n+2)
        E=x[:32]; O=x[32:]
        a_=(3**b-1)//2; b_=(3**b+1)//2
        Em=E[:,L:L+n*L]; Om=O[:,L:L+n*L]
        Omin=shf(O,-b_)*mask(-b_,j0,32,n)
        Opl=shf(O,a_)*mask(a_,j0,32,n) if a_ else Om
        Emin=shf(E,-a_)*mask(-a_,j0,32,n) if a_ else Em
        Epl=shf(E,b_)*mask(b_,j0,32,n)
        return jnp.concatenate([Omin,Em,Opl],axis=0),jnp.concatenate([Emin,Om,Epl],axis=0)
    def per_phase(w,xE,xO): return jnp.concatenate([dot(w,xE),dot(w,xO)],axis=0)
    def rowsum(v):
        s=v[:32]+v[32:]
        r=s[:,:L]
        for k in range(1,v.shape[1]//L): r=r+s[:,k*L:(k+1)*L]
        return r
    def biased(x,i):
        y=jnp.concatenate([bias[i]]*(x.shape[1]//L),axis=1)
        return x+jnp.concatenate([y,y],axis=0)
    def pc(j):
        jc=clampj(j)
        return (jc//cpp,jc%cpp) if isinstance(j,int) else (lax.div(jc,cpp),lax.rem(jc,cpp))
    def po(j):
        if isinstance(j,int): return pc(j)
        return jnp.where(j>=0,lax.div(clampj(j),cpp),packs), lax.rem(clampj(j),cpp)
    def stages(at, n):
        X={}
        jv=at[8]; jb=[at[7],at[6],at[5]]; jd=[at[2],at[3],at[4]]; ju=at[1]; jf=at[0]
        W=n*L
        def V1():
            x=ld(GU,jv-1,n+2)
            gt=cat0(x[:,L:L+W], shf(x[:32],1)*mask(1,jv,32,n), shf(x[32:],-1)*mask(-1,jv,32,n))
            y=dot(wv[...],gt)
            dU[:,:64]+=dot_nt(gt,ld(FIRST,jv,n))
            p,c=po(jv)
            sgb[p,:,pl.ds(mult(c*L),W)]=((0.2*y)*ld(DFIRST,jv,n).astype(F32)).astype(BF)
        def NT(b):
            g=ld(G[b],jb[b],n); act=ld(ACT[b],jb[b],n); hid=ld(HID[b],jb[b],n)
            dN[b,96:,:32]+=dot_nt(cat0(act[:32],hid[:32]),g[:32])+dot_nt(cat0(act[32:],hid[32:]),g[32:])
        def A(b):
            e,o=stack(GD[b],jb[b],n,b)
            g=ld(G[b],jb[b],n)
            X['A',b]=dot(wdb[b],cat0(e,g[:32])),dot(wdb[b],cat0(o,g[32:]))
            pre=ld(PRE[b],jb[b],n)
            dN[b,:96,:32]+=dot_nt(e,pre[:32])+dot_nt(o,pre[32:])
        def B2(b):
            x,y=X['A',b]
            gf=ld(DH[b],jb[b],n).astype(F32)*(0.2*cat0(x[:32],y[:32]))+cat0(x[32:],y[32:])
            gl=gf.astype(BF)
            if b==0:
                st(GU,jb[b],gl); dB[0,2]+=rowsum(gf)
            else:
                st(G[b-1],jb[b],gl); dB[b-1,1]+=rowsum(gf)
                X['g',b-1]=gl
        def AG(b):
            g=X['g',b]
            X['ag',b]=per_phase(pa[b,32:,64:],g[:32],g[32:])
        def PW(b):
            a=X['act',b]; h=ld(HID[b],jd[b],n)
            X['h',b]=per_phase(pa[b,:32,:64],cat0(a[:32],h[:32]),cat0(a[32:],h[32:]))
        def PA(b):
            a=X['act',b]; h=ld(HID[b],jd[b],n); g=X['g',b]
            x=dot(pa[b],cat0(a[:32],h[:32],g[:32])); y=dot(pa[b],cat0(a[32:],h[32:],g[32:]))
            X['h',b]=cat0(x[:32],y[:32]); X['ag',b]=cat0(x[32:],y[32:])
        def B3(b):
            gd=ld(DD[b-1],jb[b],n).astype(F32)*(0.2*X['ag',b-1])
            dB[b-1,0]+=rowsum(gd)
            st(GD[b-1],jb[b],gd)
        def D1(b):
            X['dil',b]=per_phase(wd[b],*stack(PRE[b],jd[b],n,b))
        def D2(b):
            act,dd=act_pair(biased(X['dil',b],1+2*b))
            act=act.astype(BF)
            st(ACT[b],jd[b],act)
            if b<2: st(DD[b],jd[b],dd)
            else: X['dd']=dd
            X['act',b]=act
        def G2f():
            p,c=pc(jd[2])
            gl=cot[p,:,pl.ds(mult(c*L),W)]
            st(G2,jd[2],gl)
            dB[2,1]+=rowsum(gl.astype(F32))
            X['g',2]=gl
        def D3(b):
            h=biased(X['h',b],2+2*b)
            if b<2:
                pre,dh=act_pair(h)
                st(PRE[b+1],jd[b],pre); st(HID[b+1],jd[b],h); st(DH[b+1],jd[b],dh)
            else:
                ho=h.astype(BF)
                z=cat0(*[jnp.concatenate([ho[:32,k*L:(k+1)*L],ho[32:,k*L:(k+1)*L]],axis=1) for k in range(n)])
                X['z']=dot(z,perm[...])
        def GD2f():
            gd=X['dd'].astype(F32)*(0.2*X['ag',2])
            dB[2,0]+=rowsum(gd)
            st(GD2,jd[2],gd)
        def O():
            z=X['z'].astype(BF)
            p,c=pc(jd[2])
            outb[p,:,pl.ds(mult(c*2*L),2*W)]=jnp.concatenate([z[k*32:(k+1)*32] for k in range(n)],axis=1)
        def U1():
            x=ld(FIRST,ju-1,n+2)
            fm=shf(x,-1)*mask(-1,ju,64,n); fp=shf(x,1)*mask(1,ju,64,n)
            X['u']=dot(wu[...],cat0(x[:,L:L+W],fm,fp))
        def U2():
            h=biased(X['u'],0)
            pre,dh=act_pair(h)
            st(PRE0,ju,pre); st(HID0,ju,h); st(DH0,ju,dh)
        def F():
            p,c=pc(jf if isinstance(jf,int) else jnp.minimum(jf,NCOL-n))
            fv,dv=act_pair(sig[p,:,pl.ds(mult(c*L),W)])
            st(FIRST,jf,fv); st(DFIRST,jf,dv)
        return {k: v for k,v in locals().items() if k in NAMES}
    def step(i):
        FULL(stages([i*NC-d for d in dl],NC))
    def chunks(first,end):
        return [(j,min(NC,end-j)) for j in range(first,end,NC)]
    def sweep(k,first,end,*calls):
        parts=[stages([j]*9,n) for j,n in chunks(first,end)]
        for call in calls:
            for e in parts: call(e)
    first=dl[4]//NC; last=first+NCOL//NC
    ipp=cpp//NC
    sweep(0,0,first*NC,lambda e: e["F"]())
    sweep(1,0,first*NC-dl[1],lambda e: e["U1"](),lambda e: e["U2"]())
    for b in range(2):
        sweep(2+b,0,first*NC-dl[2+b],lambda e: e["D1"](b),lambda e: e["D2"](b),lambda e: e["PW"](b),lambda e: e["D3"](b))
    done=-(-dl[8]//NC)+ipp
    assert (last-first)%UN==0
    def full(g,c):
        i=first+g*UN
        for k in range(UN):
            @pl.when((lax.rem(i-k,ipp)==done%ipp)&(i-k>=done))
            def _():
                for q in copies_out(lax.div(i-k-done,ipp)): q.start()
        for k in range(UN): step(i+k)
        return c
    lax.fori_loop(0,(last-first)//UN,full,0)
    begun=[first+g*UN-k for g in range((last-first)//UN) for k in range(UN)]
    started=[p for p in range(packs) if p*ipp+done in begun]
    out_left=range(len(started),packs)
    for p in out_left: copy_out_y(p).start()
    for b in (2,1):
        sweep(7-b,last*NC-dl[7-b],NCOL,lambda e: e["A"](b),lambda e: e["NT"](b),lambda e: e["B2"](b),lambda e: e["AG"](b-1),lambda e: e["B3"](b))
    sweep(7,last*NC-dl[7],NCOL,lambda e: e["A"](0),lambda e: e["NT"](0),lambda e: e["B2"](0))
    sweep(8,last*NC-dl[8],NCOL,lambda e: e["V1"]())
    for p in out_left: copy_out_x(p).start()
    for p in range(packs):
        for c in copies_out(p): c.wait()


def make_perm(perm, back=False):
    r=lax.broadcasted_iota(jnp.int32,(2*L,2*L),0); c=lax.broadcasted_iota(jnp.int32,(2*L,2*L),1)
    to=lambda x: jnp.where(x<L,2*x,2*(x-L)+1)
    perm[...]=((to(c)==r) if back else (to(r)==c)).astype(F32).astype(BF)


def main_call(NC, lay, signal, masks, cot, recv):
    packs,cin,T=signal.shape
    cpp=T//L
    V=pl.BlockSpec(memory_space=pltpu.VMEM); A=pl.BlockSpec(memory_space=pl.ANY)
    return pl.pallas_call(
        functools.partial(main_kernel,NC,packs,cpp,lay),
        name="section",
        out_shape=(jax.ShapeDtypeStruct((packs,32,2*T),BF),jax.ShapeDtypeStruct(signal.shape,BF),
            *[jax.ShapeDtypeStruct(x,F32) for x in ((L,L),(3,160,L),(3,3,32,L),(256,L),(2,256,L))]),
        in_specs=[V]*4, out_specs=(A,A,V,V,V,V,V),
        scratch_shapes=[pltpu.VMEM((packs,32,2*T),BF),pltpu.VMEM((packs+1,64,T),BF),
            pltpu.VMEM((7,32,L),F32),
            pltpu.SemaphoreType.DMA((2,packs))],
        compiler_params=pltpu.CompilerParams(vmem_limit_bytes=VMEM<<20),
    )(signal,masks,cot,recv)

from jax.sharding import PartitionSpec as P

MESH = pl.DeviceIdType.MESH


def peer(lay, k):
    me = lax.axis_index("dp") * lay.nf + lax.axis_index("fsdp")
    t = lax.rem(me + k, lay.n)
    return me, t, {"dp": t // lay.nf, "fsdp": lax.rem(t, lay.nf)}


def greet(lay):
    barrier = pltpu.get_barrier_semaphore()

    def hello(k, c):
        _, _, dev = peer(lay, k)
        pl.semaphore_signal(barrier, inc=1, device_id=dev, device_id_type=MESH)
        return c

    lax.fori_loop(1, lay.n, hello, 0)
    return barrier


def copy_out(lay, source, recv, send_sem, recv_sem, k):
    me, t, dev = peer(lay, k)
    return pltpu.make_async_remote_copy(
        src_ref=source(t), dst_ref=recv.at[me], send_sem=send_sem.at[k], recv_sem=recv_sem.at[k],
        device_id=dev, device_id_type=MESH)


def send(lay, *args):
    def start(k, c):
        copy_out(lay, *args, k).start()
        return c

    lax.fori_loop(1, lay.n, start, 0)


def receive(lay, *args):
    def finish(k, c):
        copy_out(lay, *args, k).wait()
        return c

    lax.fori_loop(1, lay.n, finish, 0)


def gather_kernel(lay, cot_h, *refs):
    shards_h, seg_h, (out, split, masks), shards = refs[:7], refs[7], refs[8:11], refs[11:18]
    acc, sq, msg, recv, perm, cot, seg, send_sem, recv_sem, in_sem, seg_sem, shard_sem = refs[18:]
    packs, _, width = cot_h.shape
    load = [pltpu.make_async_copy(h, v, shard_sem.at[k]) for k, (h, v) in enumerate(zip(shards_h, shards)) if v.size > 1]
    shards = [h if h.size == 1 else v for h, v in zip(shards_h, shards)]
    fetch = [pltpu.make_async_copy(cot_h.at[p], cot.at[p], in_sem.at[p]) for p in range(packs)]
    barrier = greet(lay)
    count = pltpu.make_async_copy(seg_h, seg, seg_sem)
    for c in load + [count] + fetch:
        c.start()
    acc[...] = jnp.zeros_like(acc)
    sq[...] = jnp.zeros_like(sq)
    for c in load:
        c.wait()
    ud, dd, pd, ug, ub, rg, rb = shards
    for p, o in enumerate(lay.u):
        acc[:, o:o + lay.wu] = ud[8 * p:8 * p + 8].astype(F32)
    for b in range(3):
        acc[:, lay.d[b]:lay.d[b] + lay.wd] = dd[b].astype(F32)
        for j in range(2):
            o = (2 * b + j) * lay.wp
            sq[o:o + lay.wp, 0:8] = pd[b, j].astype(F32)
        o = lay.r[b]
        acc[0:3, o:o + lay.wr] = rg[b].astype(F32)
        acc[3:6, o:o + lay.wr] = rb[b].astype(F32)
    acc[0:1, lay.g:lay.g + lay.wg] = ug[...].astype(F32)
    acc[1:2, lay.g:lay.g + lay.wr] = ub[...].astype(F32)
    full = put(acc[...], sq[...].T[:8], 0, lay.p[0], 6 * lay.wp).astype(BF)
    msg[...] = full
    me = peer(lay, 0)[0]
    recv[me] = full
    step = 8

    def part(p):
        fetch[p].wait()
        for k in range(0, width // (2 * L), step):
            x = jnp.concatenate([cot[p, :, (k + q) * 2 * L:(k + q + 1) * 2 * L] for q in range(step)], axis=0)
            z = dot(x, perm[...]).astype(BF)
            for e in range(2):
                y = jnp.concatenate([z[q * 32:(q + 1) * 32, e * L:(e + 1) * L] for q in range(step)], axis=1)
                split[p, e * 32:(e + 1) * 32, k * L:(k + step) * L] = y

    pl.semaphore_wait(barrier, lay.n - 1)
    args = (lambda t: msg, recv, send_sem, recv_sem)
    send(lay, *args)
    count.wait()
    make_masks(seg, masks, width // (2 * L))
    make_perm(perm, True)
    for p in range(packs):
        part(p)
    receive(lay, *args)
    out[...] = recv[...]


def scatter_kernel(lay, dU, dN, dB, dirs, cols, out, tmp, msgs, recv, send_sem, recv_sem):
    barrier = greet(lay)
    epilogue(lay, dU, dN, dB, dirs, cols, tmp, msgs)
    me = peer(lay, 0)[0]
    recv[me] = msgs[me]
    pl.semaphore_wait(barrier, lay.n - 1)
    args = (lambda t: msgs.at[t], recv, send_sem, recv_sem)
    send(lay, *args)
    receive(lay, *args)
    out[...] = recv[...]


def sum_kernel(lay, recv, gud, gug, gub, gdd, gpd, grg, grb):
    t = recv[0].astype(F32)
    for s in range(1, lay.n):
        t = t + recv[s].astype(F32)
    m = jnp.concatenate([move(t, lay.p[0], 0), jnp.zeros((L - 8, L), F32)], axis=0).T
    for p, o in enumerate(lay.u):
        gud[8 * p:8 * p + 8] = t[:, o:o + lay.wu]
    for b in range(3):
        gdd[b] = t[:, lay.d[b]:lay.d[b] + lay.wd]
        for j in range(2):
            o = (2 * b + j) * lay.wp
            gpd[b, j] = m[o:o + lay.wp, 0:8]
        o = lay.r[b]
        grg[b] = t[0:3, o:o + lay.wr]
        grb[b] = t[3:6, o:o + lay.wr]
    gug[...] = t[0:1, lay.g:lay.g + lay.wg]
    gub[...] = t[1:2, lay.g:lay.g + lay.wr]


def per_device(lay, signal, segments, cotangent, ud, ug, ub, dd, pd, rg, rb):
    V = pl.BlockSpec(memory_space=pltpu.VMEM)
    tiles = jax.ShapeDtypeStruct((lay.n, 8, L), BF)
    sems = [pltpu.SemaphoreType.DMA((lay.n,)), pltpu.SemaphoreType.DMA((lay.n,))]
    packs, _, width = cotangent.shape
    parted = (packs, 64, width // 2)
    H = pl.BlockSpec(memory_space=pltpu.HBM)
    shards = (ud, dd, pd.transpose(0, 1, 3, 2), ug.reshape(1, -1), ub.reshape(1, -1), rg, rb)
    table, split, masks = pl.pallas_call(
        functools.partial(gather_kernel, lay), name="gather_params", out_shape=(tiles, jax.ShapeDtypeStruct(parted, BF), jax.ShapeDtypeStruct((packs * width // (2 * L), 8, 16, L), BF)),
        in_specs=[H] + [H if v.size > 1 else V for v in shards] + [H], out_specs=(V, V, V),
        scratch_shapes=[pltpu.VMEM(v.shape, v.dtype) for v in shards] + [pltpu.VMEM((8, L), F32), pltpu.VMEM((L, L), F32), pltpu.VMEM((8, L), BF), pltpu.VMEM((lay.n, 8, L), BF),
                        pltpu.VMEM((2 * L, 2 * L), BF), pltpu.VMEM(cotangent.shape, BF), pltpu.VMEM(segments.shape, jnp.int32)] + sems
        + [pltpu.SemaphoreType.DMA((packs,)), pltpu.SemaphoreType.DMA, pltpu.SemaphoreType.DMA((7,))],
        compiler_params=pltpu.CompilerParams(collective_id=0, has_side_effects=True, vmem_limit_bytes=20 << 20),
    )(*(pltpu.with_memory_space_constraint(v, pltpu.HBM) if v.size > 1 else v for v in (cotangent, *shards, segments)))
    out, sg, *sums = main_call(NC, lay, signal, masks, split, table)
    got = pl.pallas_call(
        functools.partial(scatter_kernel, lay), name="scatter_grads", out_shape=tiles,
        in_specs=[V] * 5, out_specs=V,
        scratch_shapes=[pltpu.VMEM((6, 32, L), F32), pltpu.VMEM((lay.n, 8, L), BF), pltpu.VMEM((lay.n, 8, L), BF)] + sems,
        compiler_params=pltpu.CompilerParams(collective_id=1, has_side_effects=True, vmem_limit_bytes=4 << 20),
    )(*sums)
    f = lambda *s: jax.ShapeDtypeStruct(s, F32)
    gud, gug, gub, gdd, gpd, grg, grb = pl.pallas_call(
        functools.partial(sum_kernel, lay), name="sum_grads",
        out_shape=(f(*ud.shape), f(1, ug.shape[0]), f(1, ub.shape[0]), f(*dd.shape), f(3, 2, pd.shape[3], pd.shape[2]), f(*rg.shape), f(*rb.shape)),
        in_specs=[V], out_specs=(V,) * 7,
        compiler_params=pltpu.CompilerParams(vmem_limit_bytes=2 << 20),
    )(got)
    return out, sg, gud, gug.reshape(-1), gub.reshape(-1), gdd, gpd.transpose(0, 1, 3, 2), grg, grb


NC = 4


def solution(mesh):
    lay = Lay(mesh.shape["dp"], mesh.shape["fsdp"])
    return jax.shard_map(
        functools.partial(per_device, lay),
        mesh=mesh,
        in_specs=(
            P(("dp", "fsdp"), None, None),
            P(("dp", "fsdp"), None),
            P(("dp", "fsdp"), None, None),
            P("dp", "fsdp"),
            P("fsdp"),
            P("fsdp"),
            P(None, "dp", "fsdp"),
            P(None, None, "dp", "fsdp"),
            P(None, None, "fsdp"),
            P(None, None, "fsdp"),
        ),
        out_specs=(
            P(("dp", "fsdp"), None, None),
            P(("dp", "fsdp"), None, None),
            P("dp", "fsdp"),
            P("fsdp"),
            P("fsdp"),
            P(None, "dp", "fsdp"),
            P(None, None, "dp", "fsdp"),
            P(None, None, "fsdp"),
            P(None, None, "fsdp"),
        ),
        check_vma=False,
    )
```

time: 104 us -> 86.8 us (0.83)
  Pallas kernels: 103 us -> 85.9 us
    pallas_call x1, Pallas kernels: 79.7 us -> 63.5 us  [main_call(): pl.pallas_call(functools.partial(main_kernel, NC, packs, cpp, lay), name=...]
where the time goes in v4:
time: 86.8 us; the launch traced here: 86.6 us
  Pallas kernels  85.9 us (99%)
    pallas_call x1, Pallas kernels, main_call(): pl.pallas_call(functools.partial(main_kernel, NC, packs, cpp, lay), name=...  63.5 us
    pallas_call x1, Pallas kernels, per_device(): pl.pallas_call(functools.partial(gather_kernel, lay), name='gather_params...  12.7 us
    pallas_call x1, Pallas kernels, per_device(): pl.pallas_call(functools.partial(scatter_kernel, lay), name='scatter_grad...  8.94 us

profile of v4, /device:TPU:0, one launch (start us, length us, event | category | flops | bytes accessed | tf_op | source)
XLA Modules:
  0.0 86.6 jit_solution(1514996880855306239)
XLA Ops:
  0.6 0.0 copy-start
  0.7 12.7 %gather_params.1 = (bf16[32,8,128]{2,1,0:T(8,128)(2,1)S(1)}, bf16[8,64,4096]{2,1,0:T(8,128)(2,1)S(1)}, bf16[256,8,16,128]{3,2,1,0:T(8,128)(2,1)S(1)}) custom-call(bf16[8,32,8192]{2,1,0:T(8,128)(2,1)} %cot_h.1, bf16[16,16]{1,0:T(8,128)(2,1)} %refs_0_.1, bf16[3,8,12]{2,1,0:T(8,128)(2,1)} %refs_1_.1, bf16[3,2,4,8]{3,2,1,0:T(4,128)(2,1)} %bitcast.6, ...), custom_call_target="tpu_custom_call" | custom-call | tf_op jit(solution)/shard_map/gather_params/pallas_call | solution.py:598
  13.4 0.0 copy-done
  13.4 63.5 %section.1 = (bf16[8,32,8192]{2,1,0:T(8,128)(2,1)}, bf16[8,64,4096]{2,1,0:T(8,128)(2,1)}, f32[128,128]{1,0:T(8,128)S(1)}, f32[3,160,128]{2,1,0:T(8,128)S(1)}, f3...) custom-call(bf16[8,64,4096]{2,1,0:T(8,128)(2,1)S(1)} %copy-done, ...), custom_call_target="tpu_custom_call" | custom-call | tf_op jit(solution)/shard_map/section/pallas_call | solution.py:446
  76.9 8.9 %scatter_grads.1.recv = bf16[32,8,128]{2,1,0:T(8,128)(2,1)S(1)} custom-call(f32[128,128]{1,0:T(8,128)S(1)} %get-tuple-element.31.dU, f32[3,160,128]{2,1,0:T(8,128)S(1)} %get-tuple-element.32.dN, f32[3,3,32,128]{3,2,1,0:T(8,128)S(1)} %get-tuple-element.33.dB, f32[256,128]{1,0:T(8,128)S(1)} %get-tuple-element.34.dirs, f32[2,256,128]{2,1,0:T(8,128)S(1)} %get-tuple-element.35.cols), custom_call_target="tpu_custom_call" | custom-call | tf_op jit(solution)/shard_map/scatter_grads/pallas_call | solution.py:607
  85.8 0.8 sum_grads.1
Async XLA Ops:
  0.6 12.7 %copy-start = (bf16[8,64,4096]{2,1,0:T(8,128)(2,1)S(1)}, bf16[8,64,4096]{2,1,0:T(8,128)(2,1)}, u32[]{:S(2)}) copy-start(bf16[8,64,4096]{2,1,0:T(8,128)(2,1)} %sig.1) | copy-start | bytes 12582916

commit v5 on v4

--- a/solution.py
+++ b/solution.py
@@ -26,10 +26,10 @@
 
 def FULL(e):
     V1,NT,A,B2,AG,PW,PA,B3,D1,D2,G2f,D3,GD2f,O,U1,U2,F=[e[k] for k in NAMES]
-    NT(2); NT(1); D1(2); A(2); G2f(); D1(1); D2(2); PA(2)
-    D2(1); B2(2); A(0); A(1); D3(2); D1(0); V1(); PA(1)
-    O(); D3(1); B2(1); B2(0); B3(2); NT(0); D2(0); PA(0)
-    U1(); GD2f(); U2(); B3(1); D3(0); F()
+    G2f(); D1(2); NT(2); D2(2); A(2); D1(1); NT(1); PA(2)
+    A(1); V1(); D1(0); D2(1); B2(2); PA(1); B3(2); GD2f()
+    D3(2); B2(1); D2(0); F(); A(0); PA(0); U1(); O()
+    NT(0); B3(1); D3(1); D3(0); B2(0); U2()
 
 
 def lags(NC):
@@ -51,7 +51,7 @@
     return out
 
 
-UN=2
+UN=8
 VMEM=28
 
 

time: 86.8 us -> 81.4 us (0.938)
  Pallas kernels: 85.9 us -> 80.5 us
    pallas_call x1, Pallas kernels: 63.5 us -> 58.1 us  [main_call(): pl.pallas_call(functools.partial(main_kernel, NC, packs, cpp, lay), name=...]
where the time goes in v5:
time: 81.4 us; the launch traced here: 81.2 us
  Pallas kernels  80.5 us (99%)
    pallas_call x1, Pallas kernels, main_call(): pl.pallas_call(functools.partial(main_kernel, NC, packs, cpp, lay), name=...  58.1 us
    pallas_call x1, Pallas kernels, per_device(): pl.pallas_call(functools.partial(gather_kernel, lay), name='gather_params...  12.7 us
    pallas_call x1, Pallas kernels, per_device(): pl.pallas_call(functools.partial(scatter_kernel, lay), name='scatter_grad...  8.94 us

profile of v5, /device:TPU:0, one launch (start us, length us, event | category | flops | bytes accessed | tf_op | source)
XLA Modules:
  0.0 81.2 jit_solution(9688505680439004113)
XLA Ops:
  0.6 0.0 copy-start
  0.7 12.7 %gather_params.1 = (bf16[32,8,128]{2,1,0:T(8,128)(2,1)S(1)}, bf16[8,64,4096]{2,1,0:T(8,128)(2,1)S(1)}, bf16[256,8,16,128]{3,2,1,0:T(8,128)(2,1)S(1)}) custom-call(bf16[8,32,8192]{2,1,0:T(8,128)(2,1)} %cot_h.1, bf16[16,16]{1,0:T(8,128)(2,1)} %refs_0_.1, bf16[3,8,12]{2,1,0:T(8,128)(2,1)} %refs_1_.1, bf16[3,2,4,8]{3,2,1,0:T(4,128)(2,1)} %bitcast.6, ...), custom_call_target="tpu_custom_call" | custom-call | tf_op jit(solution)/shard_map/gather_params/pallas_call | solution.py:598
  13.4 0.0 copy-done
  13.4 58.1 %section.1 = (bf16[8,32,8192]{2,1,0:T(8,128)(2,1)}, bf16[8,64,4096]{2,1,0:T(8,128)(2,1)}, f32[128,128]{1,0:T(8,128)S(1)}, f32[3,160,128]{2,1,0:T(8,128)S(1)}, f3...) custom-call(bf16[8,64,4096]{2,1,0:T(8,128)(2,1)S(1)} %copy-done, ...), custom_call_target="tpu_custom_call" | custom-call | tf_op jit(solution)/shard_map/section/pallas_call | solution.py:446
  71.5 8.9 %scatter_grads.1.recv = bf16[32,8,128]{2,1,0:T(8,128)(2,1)S(1)} custom-call(f32[128,128]{1,0:T(8,128)S(1)} %get-tuple-element.31.dU, f32[3,160,128]{2,1,0:T(8,128)S(1)} %get-tuple-element.32.dN, f32[3,3,32,128]{3,2,1,0:T(8,128)S(1)} %get-tuple-element.33.dB, f32[256,128]{1,0:T(8,128)S(1)} %get-tuple-element.34.dirs, f32[2,256,128]{2,1,0:T(8,128)S(1)} %get-tuple-element.35.cols), custom_call_target="tpu_custom_call" | custom-call | tf_op jit(solution)/shard_map/scatter_grads/pallas_call | solution.py:607
  80.4 0.8 sum_grads.1
Async XLA Ops:
  0.6 12.7 %copy-start = (bf16[8,64,4096]{2,1,0:T(8,128)(2,1)S(1)}, bf16[8,64,4096]{2,1,0:T(8,128)(2,1)}, u32[]{:S(2)}) copy-start(bf16[8,64,4096]{2,1,0:T(8,128)(2,1)} %sig.1) | copy-start | bytes 12582916

commit v6 on v5

--- a/solution.py
+++ b/solution.py
@@ -26,10 +26,10 @@
 
 def FULL(e):
     V1,NT,A,B2,AG,PW,PA,B3,D1,D2,G2f,D3,GD2f,O,U1,U2,F=[e[k] for k in NAMES]
-    G2f(); D1(2); NT(2); D2(2); A(2); D1(1); NT(1); PA(2)
-    A(1); V1(); D1(0); D2(1); B2(2); PA(1); B3(2); GD2f()
-    D3(2); B2(1); D2(0); F(); A(0); PA(0); U1(); O()
-    NT(0); B3(1); D3(1); D3(0); B2(0); U2()
+    G2f(); D1(2); NT(2); A(2); D2(2); D1(1); NT(1); D1(0)
+    PA(2); A(1); V1(); D2(1); B2(2); PA(1); B3(2); GD2f()
+    B2(1); D2(0); D3(2); F(); A(0); PA(0); U1(); D3(1)
+    O(); NT(0); B3(1); D3(0); B2(0); U2()
 
 
 def lags(NC):

time: 81.4 us -> 79.6 us (0.978)
  Pallas kernels: 80.5 us -> 78.7 us
    pallas_call x1, Pallas kernels: 58.1 us -> 56.3 us  [main_call(): pl.pallas_call(functools.partial(main_kernel, NC, packs, cpp, lay), name=...]
where the time goes in v6:
time: 79.6 us; the launch traced here: 79.4 us
  Pallas kernels  78.7 us (99%)
    pallas_call x1, Pallas kernels, main_call(): pl.pallas_call(functools.partial(main_kernel, NC, packs, cpp, lay), name=...  56.3 us
    pallas_call x1, Pallas kernels, per_device(): pl.pallas_call(functools.partial(gather_kernel, lay), name='gather_params...  12.7 us
    pallas_call x1, Pallas kernels, per_device(): pl.pallas_call(functools.partial(scatter_kernel, lay), name='scatter_grad...  8.94 us

profile of v6, /device:TPU:0, one launch (start us, length us, event | category | flops | bytes accessed | tf_op | source)
XLA Modules:
  0.0 79.4 jit_solution(17427880789362571227)
XLA Ops:
  0.6 0.0 copy-start
  0.7 12.7 %gather_params.1 = (bf16[32,8,128]{2,1,0:T(8,128)(2,1)S(1)}, bf16[8,64,4096]{2,1,0:T(8,128)(2,1)S(1)}, bf16[256,8,16,128]{3,2,1,0:T(8,128)(2,1)S(1)}) custom-call(bf16[8,32,8192]{2,1,0:T(8,128)(2,1)} %cot_h.1, bf16[16,16]{1,0:T(8,128)(2,1)} %refs_0_.1, bf16[3,8,12]{2,1,0:T(8,128)(2,1)} %refs_1_.1, bf16[3,2,4,8]{3,2,1,0:T(4,128)(2,1)} %bitcast.6, ...), custom_call_target="tpu_custom_call" | custom-call | tf_op jit(solution)/shard_map/gather_params/pallas_call | solution.py:598
  13.4 0.0 copy-done
  13.4 56.3 %section.1 = (bf16[8,32,8192]{2,1,0:T(8,128)(2,1)}, bf16[8,64,4096]{2,1,0:T(8,128)(2,1)}, f32[128,128]{1,0:T(8,128)S(1)}, f32[3,160,128]{2,1,0:T(8,128)S(1)}, f3...) custom-call(bf16[8,64,4096]{2,1,0:T(8,128)(2,1)S(1)} %copy-done, ...), custom_call_target="tpu_custom_call" | custom-call | tf_op jit(solution)/shard_map/section/pallas_call | solution.py:446
  69.7 8.9 %scatter_grads.1.recv = bf16[32,8,128]{2,1,0:T(8,128)(2,1)S(1)} custom-call(f32[128,128]{1,0:T(8,128)S(1)} %get-tuple-element.31.dU, f32[3,160,128]{2,1,0:T(8,128)S(1)} %get-tuple-element.32.dN, f32[3,3,32,128]{3,2,1,0:T(8,128)S(1)} %get-tuple-element.33.dB, f32[256,128]{1,0:T(8,128)S(1)} %get-tuple-element.34.dirs, f32[2,256,128]{2,1,0:T(8,128)S(1)} %get-tuple-element.35.cols), custom_call_target="tpu_custom_call" | custom-call | tf_op jit(solution)/shard_map/scatter_grads/pallas_call | solution.py:607
  78.6 0.8 sum_grads.1
Async XLA Ops:
  0.6 12.7 %copy-start = (bf16[8,64,4096]{2,1,0:T(8,128)(2,1)S(1)}, bf16[8,64,4096]{2,1,0:T(8,128)(2,1)}, u32[]{:S(2)}) copy-start(bf16[8,64,4096]{2,1,0:T(8,128)(2,1)} %sig.1) | copy-start | bytes 12582916
